TPU v7x, 1024 devices: a whole 8x8x8 slice. The times are simulated.
1024 devices in a mesh: orb: 32 (over z_hi, y, core), grp: 32 (over x, z_lo).
Axes of the slice: x: 8, y: 8, z: 8 (z_hi: 2, z_lo: 4; z = z_hi * 4 + z_lo), core: 2. Of those that a mesh axis runs over, the one named last changes fastest.
Arguments:
- targets: bfloat16 [32, 98304], P('orb'), may hold values from -6 to 6
- partners: bfloat16 [2048, 98304], P(('orb', 'grp')), may hold values from -24 to 24
Outputs:
- exchange: float32 [32, 98304], P('orb', 'grp')
All inputs are finite; a program needn't handle non-finite values.
Results may differ from a plain program's by a relative error of at most 0.007.
Values may be sent and summed in bfloat16 or wider, within the bound.
No kernel may reach another device: no remote copies, remote signals or barrier semaphores. Data moves between devices by JAX's collectives and lax.ppermute only.
A program may use at most 32 MiB of HBM per device.

v0:
```python
import math

import jax
import jax.numpy as jnp
from jax import lax
from jax.sharding import PartitionSpec as P

X = 32
Y = 48
Z = 64
STEPS = 3


screening = 0.11
spacing = 0.45


def from_behind(block, axis, distance):
    devices = range(lax.axis_size(axis))
    route = [((i - distance) % len(devices), i) for i in devices]
    return lax.ppermute(block, axis, route)


def hartley(length):
    indices = jnp.arange(length, dtype=jnp.int32)
    product = indices[:, None] * indices[None, :] % length
    angles = 2.0 * math.pi / length * product.astype(jnp.float32)
    return (jnp.cos(angles) + jnp.sin(angles)).astype(jnp.bfloat16)


def block_hartley(length, copies):
    indices = jnp.arange(length * copies, dtype=jnp.int32)
    same_block = indices[:, None] // length == indices[None, :] // length
    product = indices[:, None] % length * (indices[None, :] % length) % length
    angles = 2.0 * math.pi / length * product.astype(jnp.float32)
    values = jnp.cos(angles) + jnp.sin(angles)
    return jnp.where(same_block, values, 0.0).astype(jnp.bfloat16)


def squared_wave(length):
    indices = jnp.arange(length, dtype=jnp.int32)
    folded = jnp.minimum(indices, length - indices).astype(jnp.float32)
    wavenumber = 2.0 * math.pi / (length * spacing) * folded
    return wavenumber * wavenumber


def coulomb_table():
    squares = (
        squared_wave(X)[:, None, None]
        + squared_wave(Y)[None, :, None]
        + squared_wave(Z)[None, None, :]
    )
    positive = squares > 0.0
    guarded = jnp.where(positive, squares, 1.0)
    screened = 4.0 * math.pi * (1.0 - jnp.exp(-guarded / (4.0 * screening * screening))) / guarded
    kernel = jnp.where(positive, screened, math.pi / (screening * screening))
    spread = jnp.sqrt(jnp.mean(kernel * kernel))
    return kernel / (spread * (X * Y * Z))


def contract(table, field, axis_number):
    return lax.dot_general(
        table, field, (((1,), (axis_number,)), ((), ())), preferred_element_type=jnp.float32
    ).astype(jnp.bfloat16)


def exchange_terms(target_rows, partner_rows, tables):
    table_x, table_y, block_z, kernel_table = tables
    trials = target_rows.shape[0]
    copies = partner_rows.shape[0]
    partner_grid = jnp.transpose(partner_rows.reshape(copies, X, Y, Z), (1, 2, 0, 3)).astype(
        jnp.float32
    )
    target_grid = target_rows.reshape(trials, X, Y, 1, Z).astype(jnp.float32)
    density = (
        (target_grid * partner_grid[None]).astype(jnp.bfloat16).reshape(trials, X, Y, copies * Z)
    )
    density = jnp.dot(density, block_z, preferred_element_type=jnp.float32).astype(jnp.bfloat16)
    density = contract(table_x, density, 1)
    density = contract(table_y, density, 2)
    scaled = (density.astype(jnp.float32) * kernel_table).astype(jnp.bfloat16)
    scaled = jnp.dot(scaled, block_z, preferred_element_type=jnp.float32).astype(jnp.bfloat16)
    scaled = contract(table_y, scaled, 0)
    scaled = contract(table_x, scaled, 1)
    potential = scaled.reshape(X, Y, trials, copies, Z).astype(jnp.float32)
    return jnp.sum(potential * partner_grid[:, :, None], axis=3)


def partner_sets(partners):
    received = [partners]
    for step_index in range(1, STEPS):
        received.append(from_behind(received[-1], "orb", 1))
    return received


def slab_rows(summed, trials):
    planes = summed.shape[0]
    return jnp.transpose(summed.reshape(planes, Y, trials, Z), (2, 0, 1, 3)).reshape(
        trials, planes * Y * Z
    )


def local(targets, partners):
    copies = partners.shape[0]
    trials = targets.shape[0]
    kernel_table = jnp.tile(jnp.transpose(coulomb_table(), (1, 0, 2)), (1, 1, copies))[
        :, :, None, :
    ]
    tables = (hartley(X), hartley(Y), block_hartley(Z, copies), kernel_table)
    received = partner_sets(partners)
    factor = -1.0 / math.sqrt(STEPS * lax.axis_size("grp") * copies)
    running = exchange_terms(targets, received[0], tables)
    for step_index in range(1, STEPS):
        running = running + exchange_terms(targets, received[step_index], tables)
    summed = lax.psum_scatter(
        running.reshape(X, Y * trials * Z), "grp", scatter_dimension=0, tiled=True
    )
    result = factor * slab_rows(summed, trials)
    return result


def solution(mesh):
    in_specs = (P("orb", None), P(("orb", "grp"), None))
    out_specs = P("orb", "grp")
    return jax.shard_map(local, mesh=mesh, in_specs=in_specs, out_specs=out_specs, check_vma=False)
```

profile of v0, /device:TPU:2, one launch (start us, length us, event | category | flops | bytes accessed | tf_op | source)
XLA Modules:
  0.0 419.8 jit_solution(12253647427975188097)
XLA Ops:
  6.5 2.0 collective-permute-start
  8.7 1.0 fusion.30
  9.7 1.4 reshape.351
  11.9 1.1 convert_reduce_fusion
  13.0 0.2 reshape.347
  13.2 1.1 copy.34
  14.4 18.3 %collective-permute-done = bf16[2,98304]{1,0:T(2,128)(2,1)S(1)} collective-permute-done((bf16[2,98304]{1,0:T(2,128)(2,1)}, bf16[2,98304]{1,0:T(2,128)(2,1)S(1)}, u32[]{:S(2)}, u32[]{:S(2)}) %collective-permute-start) | collective-permute-done | bytes 393248 | tf_op jit(solution)/shard_map/ppermute | solution.py:21
  32.7 1.9 collective-permute-start.1
  34.6 0.4 fusion.24
  35.0 0.9 tile.8
  35.9 1.8 tile.9
  37.7 0.4 reshape.352
  38.1 12.8 %collective-permute-done.1 = bf16[2,98304]{1,0:T(2,128)(2,1)} collective-permute-done((bf16[2,98304]{1,0:T(2,128)(2,1)S(1)}, bf16[2,98304]{1,0:T(2,128)(2,1)}, u32[]{:S(2)}, u32[]{:S(2)}) %collective-permute-start.1) | collective-permute-done | bytes 393248 | tf_op jit(solution)/shard_map/ppermute | solution.py:21
  50.9 2.6 reshape.353
  53.5 8.5 %fusion.2 = (bf16[32,48,2,64]{3,2,0,1:T(2,128)(2,1)}, bf16[32,48,2,64]{3,2,0,1:T(2,128)(2,1)}, bf16[32,48,2,64]{3,2,0,1:T(2,128)(2,1)}) fusion(f32[2,32,48,64]{3,2,1,0:T(8,128)S(1)} %reshape.352, f32[32,48,64]{2,0,1:T(8,128)} %copy.34, f32[2,32,48,64]{3,2,1,0:T(8,128)} %reshape.353, f32[2,32,48,64]{3,2,1,0:T(8,128)S(1)} %reshape.351), kind=kLoop, calls=%fused_computation.6 | loop fusion | flops 1179648 | bytes 3932160 | tf_op jit(solution)/shard_map/convert_element_type | solution.py:76
  61.9 2.1 reshape.345
  64.1 0.6 convolution_convert_fusion.11
  64.7 0.3 convolution_convert_fusion.10
  65.2 0.4 fusion.13
  65.6 0.6 convolution_convert_fusion.8
  66.2 0.4 convolution_convert_fusion.7
  66.6 1.2 fusion.10
  67.8 2.1 reshape.346
  70.0 0.6 convolution_convert_fusion.5
  70.6 0.3 convolution_convert_fusion.4
  71.1 0.4 fusion.9
  71.5 0.6 convolution_convert_fusion.2
  72.1 0.4 convolution_convert_fusion.1
  72.5 1.2 fusion.6
  73.7 2.4 reshape.344
  76.1 0.6 convolution_convert_fusion.17
  76.7 0.3 convolution_convert_fusion.16
  77.2 0.4 fusion.17
  77.6 0.6 convolution_convert_fusion.14
  78.2 0.4 convolution_convert_fusion.13
  78.6 1.2 fusion.14
  79.8 3.2 reshape.348
  83.0 5.3 %fusion.5 = f32[32,48,64]{2,0,1:T(8,128)} fusion(f32[32,48,2,64]{3,2,0,1:T(2,128)} %reshape.348, f32[2,32,48,64]{3,2,1,0:T(8,128)S(1)} %reshape.351), kind=kLoop, calls=%fused_computation.11 | loop fusion | flops 294912 | bytes 1966080 | tf_op jit(solution)/shard_map/reduce_sum | solution.py:86
  88.3 3.3 reshape.350
  91.6 5.3 %fusion.1 = f32[32,48,64]{2,0,1:T(8,128)} fusion(f32[32,48,2,64]{3,2,0,1:T(2,128)} %reshape.350, f32[2,32,48,64]{3,2,1,0:T(8,128)S(1)} %copy-done), kind=kLoop, calls=%fused_computation.3 | loop fusion | flops 294912 | bytes 1966080 | tf_op jit(solution)/shard_map/reduce_sum | solution.py:86
  96.9 2.5 reshape.349
  99.4 3.3 fusion.3
  102.8 0.2 add_add_fusion
  103.0 0.5 copy.56
  103.5 1.0 add.217
  104.5 1.3 dynamic-slice
  105.8 304.9 %all-reduce.3.cloned.1.call-done = f32[32,3072]{1,0:T(8,128)} async-done(((f32[32,3072]{1,0:T(8,128)}), f32[32,3072]{1,0:T(8,128)}) %all-reduce.3.cloned.1.call-update) | async-done | bytes 393232
  410.8 2.1 dynamic-slice_multiply_fusion
  (22 shorter events, 0.7 us)
Async XLA Ops:
  6.5 5.3 %copy-start.6 = (bf16[1,98304]{1,0:T(2,128)(2,1)S(1)}, bf16[1,98304]{1,0:T(2,128)(2,1)}, u32[]{:S(2)}) copy-start(bf16[1,98304]{1,0:T(2,128)(2,1)} %param.2) | copy-start | bytes 589828
  6.5 404.2 %all-reduce.3.cloned.1.call-start = ((), (), s32[]{:S(2)}) async-start(), calls=%async_computation | async-start | bytes 786432
  6.5 26.2 %collective-permute-start = (bf16[2,98304]{1,0:T(2,128)(2,1)}, bf16[2,98304]{1,0:T(2,128)(2,1)S(1)}, u32[]{:S(2)}, u32[]{:S(2)}) collective-permute-start(bf16[2,98304]{1,0:T(2,128)(2,1)} %param.3), channel_id=1, source_target_pairs={{992,0},{0,32},{32,64},{64,96},{96,128},{128,160},{160,192},{192,2... | collective-permute-start | bytes 1179656 | tf_op jit(solution)/shard_map/ppermute | solution.py:21
  32.7 18.2 %collective-permute-start.1 = (bf16[2,98304]{1,0:T(2,128)(2,1)S(1)}, bf16[2,98304]{1,0:T(2,128)(2,1)}, u32[]{:S(2)}, u32[]{:S(2)}) collective-permute-start(bf16[2,98304]{1,0:T(2,128)(2,1)S(1)} %collective-permute-done), channel_id=1, source_target_pairs={{992,0},{0,32},{32,64},{64,96},{96,128},{128,160},{160,192},{192,2... | collective-permute-start | bytes 1179656 | tf_op jit(solution)/shard_map/ppermute | solution.py:21
  64.1 1.1 copy-start.1
  70.0 1.1 copy-start.2
  76.1 1.1 copy-start.3
  88.3 3.3 copy-start
  99.4 3.4 copy-start.4
  99.4 3.4 copy-start.5
Sparse Core Ops, SparseCore 0:
  104.6 306.1 all-reduce.2
where the time goes:
time: 420 us
  waiting for transfers between devices  336 us (80%)
  other arithmetic  27.5 us (7%)
  local copies, waits for them, and re-layouts  27.2 us (6%)
  between operations  14.4 us (3%)
  matrix products  10.6 us (3%)
    unnamed x2, waiting for transfers between devices  305 us
    ppermute x2, waiting for transfers between devices, from_behind(): return lax.ppermute(block, axis, route)  31.1 us
    reduce_sum x3, other arithmetic, exchange_terms(): return jnp.sum(potential * partner_grid[:, :, None], axis=3)  14 us
    convert_element_type x3, local copies, waits for them, and re-layouts, exchange_terms(): potential = scaled.reshape(X, Y, trials, copies, Z).astype(jnp.float32)  8.89 us
    convert_element_type x1, other arithmetic, exchange_terms(): (target_grid * partner_grid[None]).astype(jnp.bfloat16)  8.48 us
  transfers between devices with their start and end apart: 3, of which 3 were waited for; matrix products, arithmetic and copies ran while one was open for 2% of the time, Pallas kernels for 0%

commit v1 on v0

v1 whole, which is shorter than its diff:
```python
import functools
import math

import jax
import jax.numpy as jnp
import numpy as np
from jax import lax
from jax.experimental import pallas as pl
from jax.experimental.pallas import tpu as pltpu
from jax.sharding import PartitionSpec as P

X = 32
Y = 48
Z = 64
HALF = Y // 2
STEPS = 3
XB = 4
ROWS = XB * Y
GROUPS = X // XB

screening = 0.11
spacing = 0.45

bf16 = jnp.bfloat16
f32 = jnp.float32


def hartley(length):
    indices = np.arange(length)
    angles = 2.0 * np.pi / length * (indices[:, None] * indices[None, :] % length)
    return (np.cos(angles) + np.sin(angles)).astype(np.float32)


def squared_wave(length):
    indices = np.arange(length)
    folded = np.minimum(indices, length - indices)
    return (2.0 * np.pi / (length * spacing) * folded) ** 2


def coulomb_table():
    squares = (
        squared_wave(X)[:, None, None]
        + squared_wave(Y)[None, :, None]
        + squared_wave(Z)[None, None, :]
    )
    positive = squares > 0.0
    guarded = np.where(positive, squares, 1.0)
    screened = 4.0 * np.pi * (1.0 - np.exp(-guarded / (4.0 * screening * screening))) / guarded
    kernel = np.where(positive, screened, np.pi / (screening * screening))
    spread = np.sqrt(np.mean(kernel * kernel))
    return (kernel / (spread * (X * Y * Z))).astype(np.float32)


def tables():
    order = 2 * (np.arange(Y) % HALF) + np.arange(Y) // HALF
    along_y = hartley(Y)[:, order]
    as_bf16 = lambda t: jnp.asarray(t.astype(bf16))
    z4 = as_bf16(np.kron(np.eye(4, dtype=np.float32), hartley(Z)))
    y_in = as_bf16(np.kron(np.eye(XB, dtype=np.float32), along_y))
    y_out = as_bf16(np.kron(np.eye(XB, dtype=np.float32), along_y.T))
    x8 = as_bf16(np.kron(hartley(X), np.eye(8, dtype=np.float32)))
    kernel = jnp.asarray(np.tile(coulomb_table(), (1, 1, 2)))
    return z4, y_in, y_out, x8, kernel


def low_half(shape):
    return lax.broadcasted_iota(jnp.int32, shape, len(shape) - 1) < Z


def spread_rows(first, second):
    first = first.astype(f32).reshape(XB, HALF, 2 * Z)
    second = second.astype(f32).reshape(XB, HALF, 2 * Z)
    low = low_half(first.shape)
    even = jnp.where(low, first, pltpu.roll(second, Z, 2))
    odd = jnp.where(low, pltpu.roll(first, Z, 2), second)
    return jnp.concatenate([even, odd], axis=1).reshape(ROWS, 2 * Z).astype(bf16)


def gather_rows(field):
    planes = field.reshape(XB, Y, 2 * Z)
    planes = planes + pltpu.roll(planes, Z, 2)
    even, odd = planes[:, :HALF], planes[:, HALF:]
    return jnp.where(low_half(even.shape), even, odd)


def dot(a, b):
    return jnp.dot(a, b, preferred_element_type=f32)


def middle(work, x8, kernel, lanes):
    for block in range(Y // 8):
        rows = slice(block * 8, block * 8 + 8)
        field = work[:, rows, :].reshape(X * 8, lanes).astype(bf16)
        scale = kernel[:, rows, :].reshape(X * 8, 2 * Z)
        scale = jnp.concatenate([scale] * (lanes // (2 * Z)), axis=1)
        field = dot(x8[...], field)
        field = dot(x8[...], (field * scale).astype(bf16))
        work[:, rows, :] = field.reshape(X, 8, lanes)


def own_kernel(t_ref, p_ref, z4, y_in, y_out, x8, kernel, o_ref, work, pairs):
    z2 = z4[: 2 * Z, : 2 * Z]

    def inward(step, carry):
        rows = pl.ds(pl.multiple_of(step * (XB * HALF), XB * HALF), XB * HALF)
        rows2 = pl.ds(pl.multiple_of(step * (XB * HALF) + X * HALF, XB * HALF), XB * HALF)
        trial = t_ref[rows, :]
        trial = spread_rows(trial, trial)
        partner = spread_rows(p_ref[rows, :], p_ref[rows2, :])
        planes = pl.ds(step * XB, XB)
        pairs[pl.ds(pl.multiple_of(step * ROWS, ROWS), ROWS), :] = partner
        field = dot(trial * partner, z2).astype(bf16)
        work[planes] = dot(y_in[...], field).reshape(XB, Y, 2 * Z)
        return carry

    lax.fori_loop(0, GROUPS, inward, 0)
    middle(work, x8, kernel, 2 * Z)

    def outward(step, carry):
        planes = pl.ds(step * XB, XB)
        field = work[planes].reshape(ROWS, 2 * Z).astype(bf16)
        field = dot(y_out[...], field).astype(bf16)
        field = dot(field, z2)
        partner = pairs[pl.ds(pl.multiple_of(step * ROWS, ROWS), ROWS), :].astype(f32)
        o_ref[planes] = gather_rows(field * partner)
        return carry

    lax.fori_loop(0, GROUPS, outward, 0)


def cross_kernel(
    odd_ref, t_ref, r_ref, p_ref, q_ref, own_ref, z4, y_in, y_out, x8, kernel, o_ref, work, pairs
):
    odd = odd_ref[0] == 1

    def inward(step, carry):
        rows = pl.ds(pl.multiple_of(step * (XB * HALF), XB * HALF), XB * HALF)
        rows2 = pl.ds(pl.multiple_of(step * (XB * HALF) + X * HALF, XB * HALF), XB * HALF)
        remote = r_ref[rows, :]
        chosen = jnp.where(odd, t_ref[rows, :].astype(f32), remote.astype(f32))
        trial = jnp.concatenate(
            [spread_rows(remote, remote), spread_rows(chosen, chosen)], axis=1
        )
        partner = jnp.concatenate(
            [
                spread_rows(p_ref[rows, :], p_ref[rows2, :]),
                spread_rows(q_ref[rows, :], q_ref[rows2, :]),
            ],
            axis=1,
        )
        pairs[pl.ds(pl.multiple_of(step * ROWS, ROWS), ROWS), :] = partner
        field = dot(trial * partner, z4[...]).astype(bf16)
        work[pl.ds(step * XB, XB)] = dot(y_in[...], field).reshape(XB, Y, 4 * Z)
        return carry

    lax.fori_loop(0, GROUPS, inward, 0)
    middle(work, x8, kernel, 4 * Z)

    def outward(step, carry):
        planes = pl.ds(step * XB, XB)
        field = work[planes].reshape(ROWS, 4 * Z).astype(bf16)
        field = dot(y_out[...], field).astype(bf16)
        field = dot(field, z4[...])
        field = field * pairs[pl.ds(pl.multiple_of(step * ROWS, ROWS), ROWS), :].astype(f32)
        remote = gather_rows(field[:, : 2 * Z])
        chosen = gather_rows(field[:, 2 * Z :])
        own = own_ref[planes] + jnp.where(odd, chosen, 0.0)
        remote = remote + jnp.where(odd, 0.0, chosen)
        o_ref[planes] = jnp.concatenate([own, remote], axis=1).astype(bf16)
        return carry

    lax.fori_loop(0, GROUPS, outward, 0)


VMEM = pl.BlockSpec(memory_space=pltpu.VMEM)
SMEM = pl.BlockSpec(memory_space=pltpu.SMEM)


def own_call(target, partner, tabs):
    return pl.pallas_call(
        own_kernel,
        out_shape=jax.ShapeDtypeStruct((X, HALF, 2 * Z), f32),
        in_specs=[VMEM] * 7,
        out_specs=VMEM,
        scratch_shapes=[pltpu.VMEM((X, Y, 2 * Z), f32), pltpu.VMEM((X * Y, 2 * Z), bf16)],
        cost_estimate=pl.CostEstimate(flops=2 * 10**9, bytes_accessed=2 * 10**6, transcendentals=0),
        name="own_terms",
    )(target, partner, *tabs)


def cross_call(odd, target, remote, partner, other, own, tabs):
    return pl.pallas_call(
        cross_kernel,
        out_shape=jax.ShapeDtypeStruct((X, Y, 2 * Z), bf16),
        in_specs=[SMEM] + [VMEM] * 10,
        out_specs=VMEM,
        scratch_shapes=[pltpu.VMEM((X, Y, 4 * Z), f32), pltpu.VMEM((X * Y, 4 * Z), bf16)],
        cost_estimate=pl.CostEstimate(flops=4 * 10**9, bytes_accessed=3 * 10**6, transcendentals=0),
        name="cross_terms",
    )(odd, target, remote, partner, other, own, *tabs)


def trial_route(blocks, groups, high, low):
    half = blocks // high
    pairs = []
    for block in range(blocks):
        source = (block + 2) % blocks
        for group in range(groups):
            place = group % low
            if source // half != block // half:
                place = low - 1 - place
            pairs.append((source * groups + group // low * low + place, block * groups + group))
    return pairs


def local(targets, partners):
    blocks, groups = lax.axis_size("orb"), lax.axis_size("grp")
    target = targets.reshape(X * HALF, 2 * Z)
    remote = lax.ppermute(target, ("orb", "grp"), trial_route(blocks, groups, 2, 4))
    partner = partners.reshape(2 * X * HALF, 2 * Z)
    other = lax.ppermute(partner, "orb", [(i ^ 1, i) for i in range(blocks)])
    tabs = tables()
    odd = (lax.axis_index("orb") % 2).astype(jnp.int32).reshape(1)
    own = own_call(target, partner, tabs)
    fields = cross_call(odd, target, remote, partner, other, own, tabs)
    slabs = lax.all_to_all(fields, "grp", 0, 0, tiled=True)
    summed = jnp.sum(slabs.astype(f32), axis=0)
    ahead = lax.ppermute(summed[HALF:], "orb", [(i, (i + 2) % blocks) for i in range(blocks)])
    factor = -1.0 / math.sqrt(STEPS * groups * 2)
    return ((summed[:HALF] + ahead) * factor).reshape(1, Y * Z)


def solution(mesh):
    in_specs = (P("orb", None), P(("orb", "grp"), None))
    out_specs = P("orb", "grp")
    return jax.shard_map(local, mesh=mesh, in_specs=in_specs, out_specs=out_specs, check_vma=False)
```

time: 420 us -> 80.8 us (0.19)
  waiting for transfers between devices: 336 us -> 9.68 us
  other arithmetic: 27.5 us -> 1.83 us
  local copies, waits for them, and re-layouts: 27.2 us -> 2.15 us
  blocking collectives: 0 us -> 23 us
  starting transfers between devices: 3.95 us -> 24.9 us
  Pallas kernels: 0 us -> 18.7 us
  between operations: 14.4 us -> 0.1 us
  matrix products: 10.6 us -> 0 us
    unnamed x2 -> x0, waiting for transfers between devices: 305 us -> none
    all_to_all x0 -> x1, blocking collectives: none -> 23 us  [local(): slabs = lax.all_to_all(fields, 'grp', 0, 0, tiled=True)]
    ppermute x2 -> x3, waiting for transfers between devices: 31.1 us -> 9.68 us  [the longest x1 9.68 us: local(): lax.ppermute(summed[HALF:], 'orb', [(i, (i + 2) % blocks) for i in range(...]
    ppermute x2 -> x3, starting transfers between devices: 3.95 us -> 24.9 us  [the longest x1 21 us: local(): lax.ppermute(target, ('orb', 'grp'), trial_route(blocks, groups, 2, 4))]
    pallas_call x0 -> x2, Pallas kernels: none -> 18.7 us  [the longest x1 9.72 us: cross_call(): pl.pallas_call(cross_kernel, out_shape=jax.ShapeDtypeStruct((X, Y, 2 * Z)...]
    reduce_sum x4 -> x1, other arithmetic: 15 us -> 0.07 us  [local(): summed = jnp.sum(slabs.astype(f32), axis=0)]
    convert_element_type x8 -> x0, local copies, waits for them, and re-layouts: 14.7 us -> none  [the longest x3 8.89 us: exchange_terms(): potential = scaled.reshape(X, Y, trials, copies, Z).astype(jnp.float32)]
    dot_general x18 -> x0, matrix products: 10.6 us -> none  [the longest x12 7.01 us: contract(): lax.dot_general(table, field, (((1,), (axis_number,)), ((), ())), preferr...]
  transfers between devices with their start and end apart: 3 -> 3, of which waited for: 3 -> 1; matrix products, arithmetic and copies ran while one was open for 2% -> 1% of each run, Pallas kernels for 0% -> 11%
where the time goes in v1:
time: 80.8 us; the launch traced here: 80.4 us
  starting transfers between devices  24.9 us (31%)
  blocking collectives  23 us (28%)
  Pallas kernels  18.7 us (23%)
  waiting for transfers between devices  9.68 us (12%)
  local copies, waits for them, and re-layouts  2.15 us (3%)
  other arithmetic  1.83 us (2%)
    all_to_all x1, blocking collectives, local(): slabs = lax.all_to_all(fields, 'grp', 0, 0, tiled=True)  23 us
    ppermute x1, starting transfers between devices, local(): lax.ppermute(target, ('orb', 'grp'), trial_route(blocks, groups, 2, 4))  21 us
    pallas_call x1, Pallas kernels, cross_call(): pl.pallas_call(cross_kernel, out_shape=jax.ShapeDtypeStruct((X, Y, 2 * Z)...  9.72 us
    ppermute x1, waiting for transfers between devices, local(): lax.ppermute(summed[HALF:], 'orb', [(i, (i + 2) % blocks) for i in range(...  9.68 us
    pallas_call x1, Pallas kernels, own_call(): pl.pallas_call(own_kernel, out_shape=jax.ShapeDtypeStruct((X, HALF, 2 * Z...  9.03 us
    ppermute x1, starting transfers between devices, local(): other = lax.ppermute(partner, 'orb', [(i ^ 1, i) for i in range(blocks)])  1.92 us
    ppermute x1, starting transfers between devices, local(): lax.ppermute(summed[HALF:], 'orb', [(i, (i + 2) % blocks) for i in range(...  1.92 us
  transfers between devices with their start and end apart: 3, of which 1 were waited for; matrix products, arithmetic and copies ran while one was open for 1% of the time, Pallas kernels for 11%

profile of v1, /device:TPU:2, one launch (start us, length us, event | category | flops | bytes accessed | tf_op | source)
XLA Modules:
  0.0 80.4 jit_solution(5960059124117061862)
XLA Ops:
  0.0 0.0 copy-start.1
  0.0 1.3 %reshape.14.p_ref = bf16[1536,128]{1,0:T(8,128)(2,1)S(1)} reshape(bf16[2,98304]{1,0:T(2,128)(2,1)} %param.8) | data formatting | bytes 786432 | tf_op jit(solution)/shard_map/reshape | solution.py:220
  1.3 0.0 copy-start
  1.4 1.9 %collective-permute-start.1 = (bf16[1536,128]{1,0:T(8,128)(2,1)S(1)}, bf16[1536,128]{1,0:T(8,128)(2,1)S(1)}, u32[]{:S(2)}, u32[]{:S(2)}) collective-permute-start(bf16[1536,128]{1,0:T(8,128)(2,1)S(1)} %reshape.14.p_ref), channel_id=1, source_target_pairs={{32,0},{0,32},{96,64},{64,96},{160,128},{128,160},{224,192},{192,2... | collective-permute-start | bytes 1179656 | tf_op jit(solution)/shard_map/ppermute | solution.py:221
  3.3 0.0 copy-done.1
  3.3 1.2 %reduce = bf16[98304]{0:T(1024)(128)(2,1)S(1)} reduce(bf16[1,98304]{1,0:T(2,128)(2,1)S(1)} %copy-done.1, bf16[]{:T(256)} %constant.39), dimensions={0}, to_apply=%param.7.reduce_sub_computation | reduce | bytes 393218 | tf_op args[0]
  4.5 0.0 copy-start.2
  4.5 21.0 %collective-permute-start = (bf16[768,128]{1,0:T(8,128)(2,1)S(1)}, bf16[768,128]{1,0:T(8,128)(2,1)S(1)}, u32[]{:S(2)}, u32[]{:S(2)}) collective-permute-start(bf16[768,128]{1,0:T(8,128)(2,1)S(1)} %bitcast.3), channel_id=1, source_target_pairs={{64,0},{65,1},{66,2},{67,3},{68,4},{69,5},{70,6},{71,7},{72,8},{73... | collective-permute-start | bytes 589832 | tf_op jit(solution)/shard_map/ppermute | solution.py:219
  25.5 0.0 copy-done
  25.5 0.0 copy-done.2
  25.5 9.0 %own_terms.1.own_ref = f32[32,24,128]{2,1,0:T(8,128)} custom-call(bf16[768,128]{1,0:T(8,128)(2,1)} %bitcast.4, bf16[1536,128]{1,0:T(8,128)(2,1)} %copy-done, bf16[256,256]{1,0:T(8,128)(2,1)} %constant.32.clone.z4, bf16[192,192]{1,0:T(8,128)(2,1)} %constant.33.clone.y_in, bf16[192,192]{1,0:T(8,128)(2,1)} %constant.34.clone.y_out, ...), custom_call_target="tpu_custom_call" | custom-call | flops 2000000000 | bytes 2000000 | tf_op jit(solution)/shard_map/own_terms/pallas_call | solution.py:180
  34.6 0.0 collective-permute-done.r_ref
  34.6 0.0 copy-start.4
  34.6 0.0 collective-permute-done.1.q_ref
  34.6 0.0 copy-start.3
  34.6 0.7 copy-done.4
  35.2 0.1 copy-done.3
  35.4 9.7 %cross_terms.1 = bf16[32,48,128]{2,1,0:T(8,128)(2,1)} custom-call(s32[1]{0:T(128)} %bitcast.odd_ref, bf16[768,128]{1,0:T(8,128)(2,1)} %bitcast.5, bf16[768,128]{1,0:T(8,128)(2,1)} %copy-done.4, bf16[1536,128]{1,0:T(8,128)(2,1)} %copy-done, bf16[1536,128]{1,0:T(8,128)(2,1)} %copy-done.3, f32[32,24,128]{2,1,0:T(8,128)} %own_terms.1.own_ref, ...), custom_call_target="tpu_custom_call" | custom-call | flops 4000000000 | bytes 3000000 | tf_op jit(solution)/shard_map/cross_terms/pallas_call | solution.py:192
  45.1 23.0 %all_to_all.5 = bf16[32,48,128]{2,1,0:T(8,128)(2,1)S(1)} all-to-all(bf16[32,48,128]{2,1,0:T(8,128)(2,1)} %cross_terms.1), channel_id=1, replica_groups=mesh['orb'=32,'grp'=32] {'grp'}, dimensions={0} | all-to-all | bytes 786432 | tf_op jit(solution)/shard_map/all_to_all | solution.py:226
  68.1 0.1 convert_reduce_fusion
  68.2 1.9 %collective-permute-start.2 = (f32[24,128]{1,0:T(8,128)S(1)}, f32[24,128]{1,0:T(8,128)S(1)}, u32[]{:S(2)}, u32[]{:S(2)}) collective-permute-start(f32[24,128]{1,0:T(8,128)S(1)} %slice.9), channel_id=1, source_target_pairs={{0,64},{32,96},{64,128},{96,160},{128,192},{160,224},{192,256},{22... | collective-permute-start | bytes 36872 | tf_op jit(solution)/shard_map/ppermute | solution.py:228
  70.1 9.7 %collective-permute-done.2 = f32[24,128]{1,0:T(8,128)S(1)} collective-permute-done((f32[24,128]{1,0:T(8,128)S(1)}, f32[24,128]{1,0:T(8,128)S(1)}, u32[]{:S(2)}, u32[]{:S(2)}) %collective-permute-start.2) | collective-permute-done | bytes 12320 | tf_op jit(solution)/shard_map/ppermute | solution.py:228
  79.8 0.6 fusion
  (1 shorter events, 0.0 us)
Async XLA Ops:
  0.0 3.3 %copy-start.1 = (bf16[1,98304]{1,0:T(2,128)(2,1)S(1)}, bf16[1,98304]{1,0:T(2,128)(2,1)}, u32[]{:S(2)}) copy-start(bf16[1,98304]{1,0:T(2,128)(2,1)} %param.7) | copy-start | bytes 589828
  1.3 24.2 %copy-start = (bf16[1536,128]{1,0:T(8,128)(2,1)}, bf16[1536,128]{1,0:T(8,128)(2,1)S(1)}, u32[]{:S(2)}) copy-start(bf16[1536,128]{1,0:T(8,128)(2,1)S(1)} %reshape.14.p_ref) | copy-start | bytes 1179652
  1.4 33.2 %collective-permute-start.1 = (bf16[1536,128]{1,0:T(8,128)(2,1)S(1)}, bf16[1536,128]{1,0:T(8,128)(2,1)S(1)}, u32[]{:S(2)}, u32[]{:S(2)}) collective-permute-start(bf16[1536,128]{1,0:T(8,128)(2,1)S(1)} %reshape.14.p_ref), channel_id=1, source_target_pairs={{32,0},{0,32},{96,64},{64,96},{160,128},{128,160},{224,192},{192,2... | collective-permute-start | bytes 1179656 | tf_op jit(solution)/shard_map/ppermute | solution.py:221
  4.5 21.1 %copy-start.2 = (bf16[98304]{0:T(1024)(128)(2,1)}, bf16[98304]{0:T(1024)(128)(2,1)S(1)}, u32[]{:S(2)}) copy-start(bf16[98304]{0:T(1024)(128)(2,1)S(1)} %reduce) | copy-start | bytes 589828
  4.5 30.1 %collective-permute-start = (bf16[768,128]{1,0:T(8,128)(2,1)S(1)}, bf16[768,128]{1,0:T(8,128)(2,1)S(1)}, u32[]{:S(2)}, u32[]{:S(2)}) collective-permute-start(bf16[768,128]{1,0:T(8,128)(2,1)S(1)} %bitcast.3), channel_id=1, source_target_pairs={{64,0},{65,1},{66,2},{67,3},{68,4},{69,5},{70,6},{71,7},{72,8},{73... | collective-permute-start | bytes 589832 | tf_op jit(solution)/shard_map/ppermute | solution.py:219
  34.6 0.7 copy-start.4
  34.6 0.8 copy-start.3
  68.2 11.6 %collective-permute-start.2 = (f32[24,128]{1,0:T(8,128)S(1)}, f32[24,128]{1,0:T(8,128)S(1)}, u32[]{:S(2)}, u32[]{:S(2)}) collective-permute-start(f32[24,128]{1,0:T(8,128)S(1)} %slice.9), channel_id=1, source_target_pairs={{0,64},{32,96},{64,128},{96,160},{128,192},{160,224},{192,256},{22... | collective-permute-start | bytes 36872 | tf_op jit(solution)/shard_map/ppermute | solution.py:228

commit v2 on v1

--- a/solution.py
+++ b/solution.py
@@ -1,4 +1,3 @@
-import functools
 import math
 
 import jax
@@ -113,7 +112,7 @@
         work[planes] = dot(y_in[...], field).reshape(XB, Y, 2 * Z)
         return carry
 
-    lax.fori_loop(0, GROUPS, inward, 0)
+    lax.fori_loop(0, GROUPS, inward, 0, unroll=GROUPS)
     middle(work, x8, kernel, 2 * Z)
 
     def outward(step, carry):
@@ -125,7 +124,7 @@
         o_ref[planes] = gather_rows(field * partner)
         return carry
 
-    lax.fori_loop(0, GROUPS, outward, 0)
+    lax.fori_loop(0, GROUPS, outward, 0, unroll=GROUPS)
 
 
 def cross_kernel(
@@ -153,7 +152,7 @@
         work[pl.ds(step * XB, XB)] = dot(y_in[...], field).reshape(XB, Y, 4 * Z)
         return carry
 
-    lax.fori_loop(0, GROUPS, inward, 0)
+    lax.fori_loop(0, GROUPS, inward, 0, unroll=GROUPS)
     middle(work, x8, kernel, 4 * Z)
 
     def outward(step, carry):
@@ -169,7 +168,7 @@
         o_ref[planes] = jnp.concatenate([own, remote], axis=1).astype(bf16)
         return carry
 
-    lax.fori_loop(0, GROUPS, outward, 0)
+    lax.fori_loop(0, GROUPS, outward, 0, unroll=GROUPS)
 
 
 VMEM = pl.BlockSpec(memory_space=pltpu.VMEM)
@@ -184,6 +183,7 @@
         out_specs=VMEM,
         scratch_shapes=[pltpu.VMEM((X, Y, 2 * Z), f32), pltpu.VMEM((X * Y, 2 * Z), bf16)],
         cost_estimate=pl.CostEstimate(flops=2 * 10**9, bytes_accessed=2 * 10**6, transcendentals=0),
+        compiler_params=pltpu.CompilerParams(vmem_limit_bytes=16 * 2**20),
         name="own_terms",
     )(target, partner, *tabs)
 
@@ -196,31 +196,35 @@
         out_specs=VMEM,
         scratch_shapes=[pltpu.VMEM((X, Y, 4 * Z), f32), pltpu.VMEM((X * Y, 4 * Z), bf16)],
         cost_estimate=pl.CostEstimate(flops=4 * 10**9, bytes_accessed=3 * 10**6, transcendentals=0),
+        compiler_params=pltpu.CompilerParams(vmem_limit_bytes=16 * 2**20),
         name="cross_terms",
     )(odd, target, remote, partner, other, own, *tabs)
 
 
-def trial_route(blocks, groups, high, low):
-    half = blocks // high
+LOW = 4
+
+
+def trial_route(blocks, groups):
+    half = blocks // 2
     pairs = []
     for block in range(blocks):
         source = (block + 2) % blocks
         for group in range(groups):
-            place = group % low
-            if source // half != block // half:
-                place = low - 1 - place
-            pairs.append((source * groups + group // low * low + place, block * groups + group))
+            mirror = group // LOW * LOW + LOW - 1 - group % LOW
+            place = mirror if source // half != block // half else group
+            pairs.append((source * groups + place, block * groups + group))
     return pairs
 
 
 def local(targets, partners):
     blocks, groups = lax.axis_size("orb"), lax.axis_size("grp")
+    block = lax.axis_index("orb")
     target = targets.reshape(X * HALF, 2 * Z)
-    remote = lax.ppermute(target, ("orb", "grp"), trial_route(blocks, groups, 2, 4))
+    remote = lax.ppermute(target, ("orb", "grp"), trial_route(blocks, groups))
     partner = partners.reshape(2 * X * HALF, 2 * Z)
     other = lax.ppermute(partner, "orb", [(i ^ 1, i) for i in range(blocks)])
     tabs = tables()
-    odd = (lax.axis_index("orb") % 2).astype(jnp.int32).reshape(1)
+    odd = (block % 2).astype(jnp.int32).reshape(1)
     own = own_call(target, partner, tabs)
     fields = cross_call(odd, target, remote, partner, other, own, tabs)
     slabs = lax.all_to_all(fields, "grp", 0, 0, tiled=True)

time: 80.8 us -> 72.7 us (0.90)
  Pallas kernels: 18.7 us -> 5.44 us
  waiting for transfers between devices: 9.68 us -> 15.8 us
  blocking collectives: 23 us -> 21.9 us
  other arithmetic: 1.83 us -> 2.75 us
    pallas_call x1, Pallas kernels: 9.72 us -> 2.35 us  [cross_call(): pl.pallas_call(cross_kernel, out_shape=jax.ShapeDtypeStruct((X, Y, 2 * Z)...]
    pallas_call x1, Pallas kernels: 9.03 us -> 3.09 us  [own_call(): pl.pallas_call(own_kernel, out_shape=jax.ShapeDtypeStruct((X, HALF, 2 * Z...]
    ppermute x1, waiting for transfers between devices: 0.01 us -> 3.28 us  [local(): remote = lax.ppermute(target, ('orb', 'grp'), trial_route(blocks, groups))]
    ppermute x1, waiting for transfers between devices: 9.68 us -> 12.5 us  [local(): lax.ppermute(summed[HALF:], 'orb', [(i, (i + 2) % blocks) for i in range(...]
    all_to_all x1, blocking collectives: 23 us -> 21.9 us  [local(): slabs = lax.all_to_all(fields, 'grp', 0, 0, tiled=True)]
    unnamed x1, other arithmetic: 1.16 us -> 2.08 us
  transfers between devices with their start and end apart: 3 -> 3, of which waited for: 1 -> 2; matrix products, arithmetic and copies ran while one was open for 1% -> 3% of each run, Pallas kernels for 11% -> 4%
where the time goes in v2:
time: 72.7 us; the launch traced here: 72.4 us
  starting transfers between devices  25 us (34%)
  blocking collectives  21.9 us (30%)
  waiting for transfers between devices  15.8 us (22%)
  Pallas kernels  5.44 us (7%)
  other arithmetic  2.75 us (4%)
  local copies, waits for them, and re-layouts  1.4 us (2%)
    all_to_all x1, blocking collectives, local(): slabs = lax.all_to_all(fields, 'grp', 0, 0, tiled=True)  21.9 us
    ppermute x1, starting transfers between devices, local(): remote = lax.ppermute(target, ('orb', 'grp'), trial_route(blocks, groups))  21 us
    ppermute x1, waiting for transfers between devices, local(): lax.ppermute(summed[HALF:], 'orb', [(i, (i + 2) % blocks) for i in range(...  12.5 us
    ppermute x1, waiting for transfers between devices, local(): remote = lax.ppermute(target, ('orb', 'grp'), trial_route(blocks, groups))  3.28 us
    pallas_call x1, Pallas kernels, own_call(): pl.pallas_call(own_kernel, out_shape=jax.ShapeDtypeStruct((X, HALF, 2 * Z...  3.09 us
    pallas_call x1, Pallas kernels, cross_call(): pl.pallas_call(cross_kernel, out_shape=jax.ShapeDtypeStruct((X, Y, 2 * Z)...  2.35 us
    unnamed x1, other arithmetic  2.08 us
    ppermute x1, starting transfers between devices, local(): other = lax.ppermute(partner, 'orb', [(i ^ 1, i) for i in range(blocks)])  2.05 us
  transfers between devices with their start and end apart: 3, of which 2 were waited for; matrix products, arithmetic and copies ran while one was open for 3% of the time, Pallas kernels for 4%

profile of v2, /device:TPU:2, one launch (start us, length us, event | category | flops | bytes accessed | tf_op | source)
XLA Modules:
  0.0 72.4 jit_solution(2512429676433315000)
XLA Ops:
  0.0 0.0 copy-start
  0.0 1.4 %reshape.14.p_ref = bf16[1536,128]{1,0:T(8,128)(2,1)S(1)} reshape(bf16[2,98304]{1,0:T(2,128)(2,1)} %param.8) | data formatting | bytes 786432 | tf_op jit(solution)/shard_map/reshape | solution.py:224
  1.4 0.0 copy-start.1
  1.4 0.0 copy-start.2
  1.4 0.0 copy-start.3
  1.4 0.0 copy-start.4
  1.4 2.1 %collective-permute-start.1 = (bf16[1536,128]{1,0:T(8,128)(2,1)S(1)}, bf16[1536,128]{1,0:T(8,128)(2,1)S(1)}, u32[]{:S(2)}, u32[]{:S(2)}) collective-permute-start(bf16[1536,128]{1,0:T(8,128)(2,1)S(1)} %reshape.14.p_ref), channel_id=1, source_target_pairs={{32,0},{0,32},{96,64},{64,96},{160,128},{128,160},{224,192},{192,2... | collective-permute-start | bytes 1179656 | tf_op jit(solution)/shard_map/ppermute | solution.py:225
  3.5 2.1 %reduce = bf16[98304]{0:T(1024)(128)(2,1)S(1)} reduce(bf16[1,98304]{1,0:T(2,128)(2,1)} %param.7, bf16[]{:T(256)} %constant.39), dimensions={0}, to_apply=%param.7.reduce_sub_computation | reduce | bytes 393218 | tf_op args[0]
  5.6 21.0 %collective-permute-start = (bf16[768,128]{1,0:T(8,128)(2,1)S(1)}, bf16[768,128]{1,0:T(8,128)(2,1)S(1)}, u32[]{:S(2)}, u32[]{:S(2)}) collective-permute-start(bf16[768,128]{1,0:T(8,128)(2,1)S(1)} %bitcast.3), channel_id=1, source_target_pairs={{64,0},{65,1},{66,2},{67,3},{68,4},{69,5},{70,6},{71,7},{72,8},{73... | collective-permute-start | bytes 589832 | tf_op jit(solution)/shard_map/ppermute | solution.py:223
  26.6 0.0 copy-done
  26.6 0.0 copy-done.1
  26.6 0.0 copy-done.2
  26.6 0.0 copy-done.3
  26.6 0.0 copy-done.4
  26.6 3.1 %own_terms.1.own_ref = f32[32,24,128]{2,1,0:T(8,128)S(1)} custom-call(bf16[768,128]{1,0:T(8,128)(2,1)S(1)} %bitcast.4, bf16[1536,128]{1,0:T(8,128)(2,1)S(1)} %reshape.14.p_ref, bf16[256,256]{1,0:T(8,128)(2,1)S(1)} %copy-done.2, bf16[192,192]{1,0:T(8,128)(2,1)S(1)} %copy-done.4, bf16[192,192]{1,0:T(8,128)(2,1)S(1)} %copy-done.3, ...), custom_call_target="tpu_custom_call" | custom-call | flops 2000000000 | bytes 2000000 | tf_op jit(solution)/shard_map/own_terms/pallas_call | solution.py:179
  29.8 3.3 %collective-permute-done.r_ref = bf16[768,128]{1,0:T(8,128)(2,1)S(1)} collective-permute-done((bf16[768,128]{1,0:T(8,128)(2,1)S(1)}, bf16[768,128]{1,0:T(8,128)(2,1)S(1)}, u32[]{:S(2)}, u32[]{:S(2)}) %collective-permute-start) | collective-permute-done | bytes 196640 | tf_op jit(solution)/shard_map/ppermute | solution.py:223
  33.0 0.0 collective-permute-done.1.q_ref
  33.0 2.3 %cross_terms.1 = bf16[32,48,128]{2,1,0:T(8,128)(2,1)S(1)} custom-call(s32[1]{0:T(128)} %bitcast.odd_ref, bf16[768,128]{1,0:T(8,128)(2,1)S(1)} %bitcast.5, bf16[768,128]{1,0:T(8,128)(2,1)S(1)} %collective-permute-done.r_ref, bf16[1536,128]{1,0:T(8,128)(2,1)S(1)} %reshape.14.p_ref, bf16[1536,128]{1,0:T(8,128)(2,1)S(1)} %collective-permute-done.1.q_ref, ...), custom_call_target="tpu_custom_call" | custom-call | flops 4000000000 | bytes 3000000 | tf_op jit(solution)/shard_map/cross_terms/pallas_call | solution.py:192
  35.4 21.9 %all_to_all.5 = bf16[32,48,128]{2,1,0:T(8,128)(2,1)S(1)} all-to-all(bf16[32,48,128]{2,1,0:T(8,128)(2,1)S(1)} %cross_terms.1), channel_id=1, replica_groups=mesh['orb'=32,'grp'=32] {'grp'}, dimensions={0} | all-to-all | bytes 786432 | tf_op jit(solution)/shard_map/all_to_all | solution.py:230
  57.3 0.1 convert_reduce_fusion
  57.4 1.9 %collective-permute-start.2 = (f32[24,128]{1,0:T(8,128)S(1)}, f32[24,128]{1,0:T(8,128)S(1)}, u32[]{:S(2)}, u32[]{:S(2)}) collective-permute-start(f32[24,128]{1,0:T(8,128)S(1)} %slice.9), channel_id=1, source_target_pairs={{0,64},{32,96},{64,128},{96,160},{128,192},{160,224},{192,256},{22... | collective-permute-start | bytes 36872 | tf_op jit(solution)/shard_map/ppermute | solution.py:232
  59.3 12.5 %collective-permute-done.2 = f32[24,128]{1,0:T(8,128)S(1)} collective-permute-done((f32[24,128]{1,0:T(8,128)S(1)}, f32[24,128]{1,0:T(8,128)S(1)}, u32[]{:S(2)}, u32[]{:S(2)}) %collective-permute-start.2) | collective-permute-done | bytes 12320 | tf_op jit(solution)/shard_map/ppermute | solution.py:232
  71.8 0.6 fusion
  (1 shorter events, 0.0 us)
Async XLA Ops:
  0.0 26.6 %copy-start = (f32[32,48,128]{2,1,0:T(8,128)S(1)}, f32[32,48,128]{2,1,0:T(8,128)}, u32[]{:S(2)}) copy-start(f32[32,48,128]{2,1,0:T(8,128)} %constant.36.clone.kernel) | copy-start | bytes 2359300
  1.4 25.2 %copy-start.1 = (bf16[256,256]{1,0:T(8,128)(2,1)S(1)}, bf16[256,256]{1,0:T(8,128)(2,1)}, u32[]{:S(2)}) copy-start(bf16[256,256]{1,0:T(8,128)(2,1)} %constant.35.clone.x8) | copy-start | bytes 393220
  1.4 25.2 %copy-start.2 = (bf16[256,256]{1,0:T(8,128)(2,1)S(1)}, bf16[256,256]{1,0:T(8,128)(2,1)}, u32[]{:S(2)}) copy-start(bf16[256,256]{1,0:T(8,128)(2,1)} %constant.32.clone.z4) | copy-start | bytes 393220
  1.4 25.2 %copy-start.3 = (bf16[192,192]{1,0:T(8,128)(2,1)S(1)}, bf16[192,192]{1,0:T(8,128)(2,1)}, u32[]{:S(2)}) copy-start(bf16[192,192]{1,0:T(8,128)(2,1)} %constant.34.clone.y_out) | copy-start | bytes 221188
  1.4 25.2 %copy-start.4 = (bf16[192,192]{1,0:T(8,128)(2,1)S(1)}, bf16[192,192]{1,0:T(8,128)(2,1)}, u32[]{:S(2)}) copy-start(bf16[192,192]{1,0:T(8,128)(2,1)} %constant.33.clone.y_in) | copy-start | bytes 221188
  1.4 31.6 %collective-permute-start.1 = (bf16[1536,128]{1,0:T(8,128)(2,1)S(1)}, bf16[1536,128]{1,0:T(8,128)(2,1)S(1)}, u32[]{:S(2)}, u32[]{:S(2)}) collective-permute-start(bf16[1536,128]{1,0:T(8,128)(2,1)S(1)} %reshape.14.p_ref), channel_id=1, source_target_pairs={{32,0},{0,32},{96,64},{64,96},{160,128},{128,160},{224,192},{192,2... | collective-permute-start | bytes 1179656 | tf_op jit(solution)/shard_map/ppermute | solution.py:225
  5.6 27.5 %collective-permute-start = (bf16[768,128]{1,0:T(8,128)(2,1)S(1)}, bf16[768,128]{1,0:T(8,128)(2,1)S(1)}, u32[]{:S(2)}, u32[]{:S(2)}) collective-permute-start(bf16[768,128]{1,0:T(8,128)(2,1)S(1)} %bitcast.3), channel_id=1, source_target_pairs={{64,0},{65,1},{66,2},{67,3},{68,4},{69,5},{70,6},{71,7},{72,8},{73... | collective-permute-start | bytes 589832 | tf_op jit(solution)/shard_map/ppermute | solution.py:223
  57.4 14.4 %collective-permute-start.2 = (f32[24,128]{1,0:T(8,128)S(1)}, f32[24,128]{1,0:T(8,128)S(1)}, u32[]{:S(2)}, u32[]{:S(2)}) collective-permute-start(f32[24,128]{1,0:T(8,128)S(1)} %slice.9), channel_id=1, source_target_pairs={{0,64},{32,96},{64,128},{96,160},{128,192},{160,224},{192,256},{22... | collective-permute-start | bytes 36872 | tf_op jit(solution)/shard_map/ppermute | solution.py:232

commit v3 on v2

v3 whole, which is shorter than its diff:
```python
import math

import jax
import jax.numpy as jnp
import numpy as np
from jax import lax
from jax.experimental import pallas as pl
from jax.experimental.pallas import tpu as pltpu
from jax.sharding import PartitionSpec as P

X = 32
Y = 48
Z = 64
HALF = Y // 2
STEPS = 3
XB = 4
ROWS = XB * Y
GROUPS = X // XB
SIDE = 256

screening = 0.11
spacing = 0.45

bf16 = jnp.bfloat16
f32 = jnp.float32


def hartley(length):
    indices = np.arange(length)
    angles = 2.0 * np.pi / length * (indices[:, None] * indices[None, :] % length)
    return (np.cos(angles) + np.sin(angles)).astype(np.float32)


def squared_wave(length):
    indices = np.arange(length)
    folded = np.minimum(indices, length - indices)
    return (2.0 * np.pi / (length * spacing) * folded) ** 2


def coulomb_table():
    squares = (
        squared_wave(X)[:, None, None]
        + squared_wave(Y)[None, :, None]
        + squared_wave(Z)[None, None, :]
    )
    positive = squares > 0.0
    guarded = np.where(positive, squares, 1.0)
    screened = 4.0 * np.pi * (1.0 - np.exp(-guarded / (4.0 * screening * screening))) / guarded
    kernel = np.where(positive, screened, np.pi / (screening * screening))
    spread = np.sqrt(np.mean(kernel * kernel))
    return (kernel / (spread * (X * Y * Z))).astype(np.float32)


def tables():
    order = 2 * (np.arange(Y) % HALF) + np.arange(Y) // HALF
    along_y = hartley(Y)[:, order]
    joined = np.zeros((SIDE, 4 * SIDE), np.float32)
    joined[:, :SIDE] = np.kron(np.eye(4, dtype=np.float32), hartley(Z))
    joined[:, SIDE : 2 * SIDE] = np.kron(hartley(X), np.eye(8, dtype=np.float32))
    joined[:ROWS, 2 * SIDE : 2 * SIDE + ROWS] = np.kron(np.eye(XB, dtype=np.float32), along_y)
    joined[:ROWS, 3 * SIDE : 3 * SIDE + ROWS] = np.kron(np.eye(XB, dtype=np.float32), along_y.T)
    kernel = jnp.asarray(np.tile(coulomb_table(), (1, 1, 2)))
    return jnp.asarray(joined.astype(bf16)), kernel


def views(joined):
    return (
        joined.at[:, :SIDE],
        joined.at[:, SIDE : 2 * SIDE],
        joined.at[:ROWS, 2 * SIDE : 2 * SIDE + ROWS],
        joined.at[:ROWS, 3 * SIDE : 3 * SIDE + ROWS],
    )


def low_half(shape):
    return lax.broadcasted_iota(jnp.int32, shape, len(shape) - 1) < Z


def spread_rows(first, second):
    first = first.astype(f32).reshape(XB, HALF, 2 * Z)
    second = second.astype(f32).reshape(XB, HALF, 2 * Z)
    low = low_half(first.shape)
    even = jnp.where(low, first, pltpu.roll(second, Z, 2))
    odd = jnp.where(low, pltpu.roll(first, Z, 2), second)
    return jnp.concatenate([even, odd], axis=1).reshape(ROWS, 2 * Z).astype(bf16)


def gather_rows(field):
    planes = field.reshape(XB, Y, 2 * Z)
    planes = planes + pltpu.roll(planes, Z, 2)
    even, odd = planes[:, :HALF], planes[:, HALF:]
    return jnp.where(low_half(even.shape), even, odd)


def dot(a, b):
    return jnp.dot(a, b, preferred_element_type=f32)


def middle(work, x8, kernel, lanes):
    for block in range(Y // 8):
        rows = slice(block * 8, block * 8 + 8)
        field = work[:, rows, :].reshape(X * 8, lanes).astype(bf16)
        scale = kernel[:, rows, :].reshape(X * 8, 2 * Z)
        scale = jnp.concatenate([scale] * (lanes // (2 * Z)), axis=1)
        field = dot(x8[...], field)
        field = dot(x8[...], (field * scale).astype(bf16))
        work[:, rows, :] = field.reshape(X, 8, lanes)


def chunk(step, high, base=0):
    return pl.ds(pl.multiple_of(step * high + base, high), high)


def density(trial, partner):
    trial = spread_rows(trial, trial)
    return jnp.concatenate([trial * partner[:, : 2 * Z], trial * partner[:, 2 * Z :]], axis=1)


def inward(field, z4, y_in):
    return dot(y_in[...], dot(field, z4[...]).astype(bf16)).reshape(XB, Y, 4 * Z)


def outward(work, step, partner, both, z4, y_out):
    field = work[pl.ds(step * XB, XB)].reshape(ROWS, 4 * Z).astype(bf16)
    field = dot(dot(y_out[...], field).astype(bf16), z4[...]) * partner.astype(f32)
    return gather_rows(field[:, : 2 * Z] + jnp.where(both, field[:, 2 * Z :], 0.0))


def own_kernel(
    odd_ref, t_ref, p_ref, q_ref, joined, kernel, o_ref, pairs, work
):
    z4, x8, y_in, y_out = views(joined)
    odd = odd_ref[0] == 1
    high = XB * HALF
    for step in range(GROUPS):
        rows, rows2 = chunk(step, high), chunk(step, high, X * HALF)
        partner = jnp.concatenate(
            [
                spread_rows(p_ref[rows, :], p_ref[rows2, :]),
                spread_rows(q_ref[rows, :], q_ref[rows2, :]),
            ],
            axis=1,
        )
        pairs[chunk(step, ROWS), :] = partner
        work[pl.ds(step * XB, XB)] = inward(density(t_ref[rows, :], partner), z4, y_in)
    middle(work, x8, kernel, 4 * Z)
    for step in range(GROUPS):
        partner = pairs[chunk(step, ROWS), :]
        o_ref[pl.ds(step * XB, XB)] = outward(work, step, partner, odd, z4, y_out)


def cross_kernel(
    odd_ref, t_ref, pairs, own_ref, joined, kernel, o_ref, work
):
    z4, x8, y_in, y_out = views(joined)
    even = odd_ref[0] == 0
    for step in range(GROUPS):
        partner = pairs[chunk(step, ROWS), :]
        field = density(t_ref[chunk(step, XB * HALF), :], partner)
        work[pl.ds(step * XB, XB)] = inward(field, z4, y_in)
    middle(work, x8, kernel, 4 * Z)
    for step in range(GROUPS):
        partner = pairs[chunk(step, ROWS), :]
        cross = outward(work, step, partner, even, z4, y_out)
        planes = pl.ds(step * XB, XB)
        o_ref[planes] = jnp.concatenate([own_ref[planes], cross], axis=1).astype(bf16)


def rows_kernel(x_ref, o_ref):
    o_ref[...] = x_ref[...].reshape(o_ref.shape)


PARTS = 4


def split_rows_kernel(x_ref, o_ref, landed, sems):
    width = x_ref.shape[1] // PARTS
    high = o_ref.shape[0] // PARTS
    copies = []
    for part in range(PARTS):
        columns = slice(part * width, (part + 1) * width)
        copies.append(
            pltpu.make_async_copy(x_ref.at[:, columns], landed.at[:, columns], sems.at[part])
        )
        copies[-1].start()
    for part, copy in enumerate(copies):
        copy.wait()
        field = landed[:, part * width : (part + 1) * width]
        o_ref[part * high : (part + 1) * high, :] = field.reshape(high, 2 * Z)


VMEM = pl.BlockSpec(memory_space=pltpu.VMEM)
SMEM = pl.BlockSpec(memory_space=pltpu.SMEM)
GRANT = pltpu.CompilerParams(vmem_limit_bytes=16 * 2**20)


def as_rows(fields):
    return pl.pallas_call(
        rows_kernel,
        out_shape=jax.ShapeDtypeStruct((fields.shape[0] * X * HALF, 2 * Z), bf16),
        in_specs=[VMEM],
        out_specs=VMEM,
        cost_estimate=pl.CostEstimate(flops=0, bytes_accessed=10**6, transcendentals=0),
        compiler_params=GRANT,
        name="as_rows",
    )(fields)


def as_rows_early(fields):
    return pl.pallas_call(
        split_rows_kernel,
        out_shape=jax.ShapeDtypeStruct((fields.shape[0] * X * HALF, 2 * Z), bf16),
        in_specs=[pl.BlockSpec(memory_space=pltpu.HBM)],
        out_specs=VMEM,
        scratch_shapes=[pltpu.VMEM(fields.shape, bf16), pltpu.SemaphoreType.DMA((PARTS,))],
        cost_estimate=pl.CostEstimate(flops=0, bytes_accessed=10**6, transcendentals=0),
        compiler_params=GRANT,
        name="as_rows_early",
    )(fields)


COST = pl.CostEstimate(flops=4 * 10**9, bytes_accessed=3 * 10**6, transcendentals=0)
WORK = pltpu.VMEM((X, Y, 4 * Z), f32)


def own_call(odd, trial, partner, other, tabs):
    return pl.pallas_call(
        own_kernel,
        out_shape=(
            jax.ShapeDtypeStruct((X, HALF, 2 * Z), f32),
            jax.ShapeDtypeStruct((X * Y, 4 * Z), bf16),
        ),
        in_specs=[SMEM] + [VMEM] * 5,
        out_specs=(VMEM, VMEM),
        scratch_shapes=[WORK],
        cost_estimate=COST,
        compiler_params=GRANT,
        name="own_terms",
    )(odd, trial, partner, other, *tabs)


def cross_call(odd, trial, pairs, own, tabs):
    return pl.pallas_call(
        cross_kernel,
        out_shape=jax.ShapeDtypeStruct((X, Y, 2 * Z), bf16),
        in_specs=[SMEM] + [VMEM] * 5,
        out_specs=VMEM,
        scratch_shapes=[WORK],
        cost_estimate=COST,
        compiler_params=GRANT,
        name="cross_terms",
    )(odd, trial, pairs, own, *tabs)


LOW = 4


def trial_route(blocks, groups):
    half = blocks // 2
    pairs = []
    for block in range(blocks):
        source = (block + 2) % blocks
        for group in range(groups):
            place = group % LOW
            if source // half != block // half:
                if block % 2 == 0:
                    place = LOW - 1 - place
                else:
                    place = (place + (1 if block >= half else LOW - 1)) % LOW
            pairs.append((source * groups + group // LOW * LOW + place, block * groups + group))
    return pairs


def local(targets, partners):
    blocks, groups = lax.axis_size("orb"), lax.axis_size("grp")
    block = lax.axis_index("orb")
    target = as_rows_early(targets)
    remote = lax.ppermute(target, ("orb", "grp"), trial_route(blocks, groups))
    partner = as_rows(partners)
    other = lax.ppermute(partner, "orb", [(i ^ 1, i) for i in range(blocks)])
    tabs = tables()
    odd = (block % 2).astype(jnp.int32).reshape(1)
    own, pairs = own_call(odd, target, partner, other, tabs)
    fields = cross_call(odd, remote, pairs, own, tabs)
    slabs = lax.all_to_all(fields, "grp", 0, 0, tiled=True)
    summed = jnp.sum(slabs.astype(f32), axis=0)
    ahead = lax.ppermute(summed[HALF:], "orb", [(i, (i + 2) % blocks) for i in range(blocks)])
    factor = -1.0 / math.sqrt(STEPS * groups * 2)
    return ((summed[:HALF] + ahead) * factor).reshape(1, Y * Z)


def solution(mesh):
    in_specs = (P("orb", None), P(("orb", "grp"), None))
    out_specs = P("orb", "grp")
    return jax.shard_map(local, mesh=mesh, in_specs=in_specs, out_specs=out_specs, check_vma=False)
```

time: 72.7 us -> 69.1 us (0.950)
  waiting for transfers between devices: 15.8 us -> 13 us
  other arithmetic: 2.75 us -> 0.67 us
  blocking collectives: 21.9 us -> 22.7 us
    ppermute x1, waiting for transfers between devices: 12.5 us -> 10.3 us  [local(): lax.ppermute(summed[HALF:], 'orb', [(i, (i + 2) % blocks) for i in range(...]
    unnamed x1 -> x0, other arithmetic: 2.08 us -> none
    unnamed x10, local copies, waits for them, and re-layouts: 0.03 us -> 2.04 us
    reshape x1 -> x0, local copies, waits for them, and re-layouts: 1.36 us -> none  [local(): partner = partners.reshape(2 * X * HALF, 2 * Z)]
    all_to_all x1, blocking collectives: 21.9 us -> 22.7 us  [local(): slabs = lax.all_to_all(fields, 'grp', 0, 0, tiled=True)]
    pallas_call x1 -> x3, Pallas kernels: 3.09 us -> 3 us  [the longest x1 2.36 us: own_call(): pl.pallas_call(own_kernel, out_shape=(jax.ShapeDtypeStruct((X, HALF, 2 *...]
  transfers between devices with their start and end apart: 3 -> 3, of which waited for: 2 -> 2; matrix products, arithmetic and copies ran while one was open for 3% -> 0% of each run, Pallas kernels for 4% -> 4%
where the time goes in v3:
time: 69.1 us; the launch traced here: 68.8 us
  starting transfers between devices  25 us (36%)
  blocking collectives  22.7 us (33%)
  waiting for transfers between devices  13 us (19%)
  Pallas kernels  5.32 us (8%)
  local copies, waits for them, and re-layouts  2.05 us (3%)
    all_to_all x1, blocking collectives, local(): slabs = lax.all_to_all(fields, 'grp', 0, 0, tiled=True)  22.7 us
    ppermute x1, starting transfers between devices, local(): remote = lax.ppermute(target, ('orb', 'grp'), trial_route(blocks, groups))  21 us
    ppermute x1, waiting for transfers between devices, local(): lax.ppermute(summed[HALF:], 'orb', [(i, (i + 2) % blocks) for i in range(...  10.3 us
    ppermute x1, waiting for transfers between devices, local(): remote = lax.ppermute(target, ('orb', 'grp'), trial_route(blocks, groups))  2.69 us
    pallas_call x1, Pallas kernels, own_call(): pl.pallas_call(own_kernel, out_shape=(jax.ShapeDtypeStruct((X, HALF, 2 *...  2.36 us
    pallas_call x1, Pallas kernels, cross_call(): pl.pallas_call(cross_kernel, out_shape=jax.ShapeDtypeStruct((X, Y, 2 * Z)...  2.32 us
    ppermute x1, starting transfers between devices, local(): other = lax.ppermute(partner, 'orb', [(i ^ 1, i) for i in range(blocks)])  2.05 us
    unnamed x10, local copies, waits for them, and re-layouts  2.04 us
  transfers between devices with their start and end apart: 3, of which 2 were waited for; matrix products, arithmetic and copies ran while one was open for 0% of the time, Pallas kernels for 4%

profile of v3, /device:TPU:2, one launch (start us, length us, event | category | flops | bytes accessed | tf_op | source)
XLA Modules:
  0.0 68.8 jit_solution(12231357972705314824)
XLA Ops:
  0.0 0.0 copy-start
  0.0 1.0 %copy-done = bf16[2,98304]{1,0:T(2,128)(2,1)S(1)} copy-done((bf16[2,98304]{1,0:T(2,128)(2,1)S(1)}, bf16[2,98304]{1,0:T(2,128)(2,1)}, u32[]{:S(2)}) %copy-start) | copy-done | bytes 393240
  1.0 0.0 copy-start.1
  1.0 0.0 copy-start.2
  1.0 0.1 as_rows.1.p_ref
  1.1 2.1 %collective-permute-start.1 = (bf16[1536,128]{1,0:T(8,128)(2,1)S(1)}, bf16[1536,128]{1,0:T(8,128)(2,1)S(1)}, u32[]{:S(2)}, u32[]{:S(2)}) collective-permute-start(bf16[1536,128]{1,0:T(8,128)(2,1)S(1)} %as_rows.1.p_ref), channel_id=1, source_target_pairs={{32,0},{0,32},{96,64},{64,96},{160,128},{128,160},{224,192},{192,2... | collective-permute-start | bytes 1179656 | tf_op jit(solution)/shard_map/ppermute | solution.py:280
  3.1 0.0 copy-done.1
  3.1 0.6 as_rows_early.1.t_ref
  3.7 21.0 %collective-permute-start = (bf16[768,128]{1,0:T(8,128)(2,1)S(1)}, bf16[768,128]{1,0:T(8,128)(2,1)S(1)}, u32[]{:S(2)}, u32[]{:S(2)}) collective-permute-start(bf16[768,128]{1,0:T(8,128)(2,1)S(1)} %as_rows_early.1.t_ref), channel_id=1, source_target_pairs={{64,0},{65,1},{66,2},{67,3},{68,4},{69,5},{70,6},{71,7},{72,8},{73... | collective-permute-start | bytes 589832 | tf_op jit(solution)/shard_map/ppermute | solution.py:278
  24.8 0.0 collective-permute-done.1.q_ref
  24.8 0.0 copy-done.2
  24.8 0.0 copy-start.3
  24.8 1.0 %copy-done.3 = bf16[256,1024]{1,0:T(8,128)(2,1)S(1)} copy-done((bf16[256,1024]{1,0:T(8,128)(2,1)S(1)}, bf16[256,1024]{1,0:T(8,128)(2,1)}, u32[]{:S(2)}) %copy-start.3) | copy-done | bytes 524312
  25.8 0.0 copy-start.4
  25.8 2.4 %own_terms.1 = (f32[32,24,128]{2,1,0:T(8,128)S(1)}, bf16[1536,256]{1,0:T(8,128)(2,1)S(1)}) custom-call(s32[1]{0:T(128)} %bitcast.odd_ref, bf16[768,128]{1,0:T(8,128)(2,1)S(1)} %as_rows_early.1.t_ref, bf16[1536,128]{1,0:T(8,128)(2,1)S(1)} %as_rows.1.p_ref, bf16[1536,128]{1,0:T(8,128)(2,1)S(1)} %collective-permute-done.1.q_ref, ...), custom_call_target="tpu_custom_call" | custom-call | flops 4000000000 | bytes 3000000 | tf_op jit(solution)/shard_map/own_terms/pallas_call | solution.py:227
  28.2 2.7 %collective-permute-done.t_ref = bf16[768,128]{1,0:T(8,128)(2,1)S(1)} collective-permute-done((bf16[768,128]{1,0:T(8,128)(2,1)S(1)}, bf16[768,128]{1,0:T(8,128)(2,1)S(1)}, u32[]{:S(2)}, u32[]{:S(2)}) %collective-permute-start) | collective-permute-done | bytes 196640 | tf_op jit(solution)/shard_map/ppermute | solution.py:278
  30.9 0.0 copy-done.4
  30.9 2.3 %cross_terms.1 = bf16[32,48,128]{2,1,0:T(8,128)(2,1)S(1)} custom-call(s32[1]{0:T(128)} %bitcast.odd_ref, bf16[768,128]{1,0:T(8,128)(2,1)S(1)} %collective-permute-done.t_ref, bf16[1536,256]{1,0:T(8,128)(2,1)S(1)} %get-tuple-element.7.pairs, f32[32,24,128]{2,1,0:T(8,128)S(1)} %get-tuple-element.8.own_ref, bf16[256,1024]{1,0:T(8,128)(2,1)S(1)} %copy-done.4, ...), custom_call_target="tpu_custom_call" | custom-call | flops 4000000000 | bytes 3000000 | tf_op jit(solution)/shard_map/cross_terms/pallas_call | solution.py:243
  33.2 22.7 %all_to_all.5 = bf16[32,48,128]{2,1,0:T(8,128)(2,1)S(1)} all-to-all(bf16[32,48,128]{2,1,0:T(8,128)(2,1)S(1)} %cross_terms.1), channel_id=1, replica_groups=mesh['orb'=32,'grp'=32] {'grp'}, dimensions={0} | all-to-all | bytes 786432 | tf_op jit(solution)/shard_map/all_to_all | solution.py:285
  55.9 0.1 convert_reduce_fusion
  55.9 1.9 %collective-permute-start.2 = (f32[24,128]{1,0:T(8,128)S(1)}, f32[24,128]{1,0:T(8,128)S(1)}, u32[]{:S(2)}, u32[]{:S(2)}) collective-permute-start(f32[24,128]{1,0:T(8,128)S(1)} %slice.9), channel_id=1, source_target_pairs={{0,64},{32,96},{64,128},{96,160},{128,192},{160,224},{192,256},{22... | collective-permute-start | bytes 36872 | tf_op jit(solution)/shard_map/ppermute | solution.py:287
  57.9 10.3 %collective-permute-done.2 = f32[24,128]{1,0:T(8,128)S(1)} collective-permute-done((f32[24,128]{1,0:T(8,128)S(1)}, f32[24,128]{1,0:T(8,128)S(1)}, u32[]{:S(2)}, u32[]{:S(2)}) %collective-permute-start.2) | collective-permute-done | bytes 12320 | tf_op jit(solution)/shard_map/ppermute | solution.py:287
  68.2 0.6 fusion
  (1 shorter events, 0.0 us)
Async XLA Ops:
  0.0 1.0 %copy-start = (bf16[2,98304]{1,0:T(2,128)(2,1)S(1)}, bf16[2,98304]{1,0:T(2,128)(2,1)}, u32[]{:S(2)}) copy-start(bf16[2,98304]{1,0:T(2,128)(2,1)} %x_ref.3) | copy-start | bytes 1179652
  1.0 2.1 %copy-start.1 = (bf16[1,98304]{1,0:T(2,128)(2,1)S(1)}, bf16[1,98304]{1,0:T(2,128)(2,1)}, u32[]{:S(2)}) copy-start(bf16[1,98304]{1,0:T(2,128)(2,1)} %x_ref.2) | copy-start | bytes 589828
  1.0 23.8 %copy-start.2 = (f32[32,48,128]{2,1,0:T(8,128)S(1)}, f32[32,48,128]{2,1,0:T(8,128)}, u32[]{:S(2)}) copy-start(f32[32,48,128]{2,1,0:T(8,128)} %constant.26.clone.kernel) | copy-start | bytes 2359300
  1.1 23.7 %collective-permute-start.1 = (bf16[1536,128]{1,0:T(8,128)(2,1)S(1)}, bf16[1536,128]{1,0:T(8,128)(2,1)S(1)}, u32[]{:S(2)}, u32[]{:S(2)}) collective-permute-start(bf16[1536,128]{1,0:T(8,128)(2,1)S(1)} %as_rows.1.p_ref), channel_id=1, source_target_pairs={{32,0},{0,32},{96,64},{64,96},{160,128},{128,160},{224,192},{192,2... | collective-permute-start | bytes 1179656 | tf_op jit(solution)/shard_map/ppermute | solution.py:280
  3.7 27.2 %collective-permute-start = (bf16[768,128]{1,0:T(8,128)(2,1)S(1)}, bf16[768,128]{1,0:T(8,128)(2,1)S(1)}, u32[]{:S(2)}, u32[]{:S(2)}) collective-permute-start(bf16[768,128]{1,0:T(8,128)(2,1)S(1)} %as_rows_early.1.t_ref), channel_id=1, source_target_pairs={{64,0},{65,1},{66,2},{67,3},{68,4},{69,5},{70,6},{71,7},{72,8},{73... | collective-permute-start | bytes 589832 | tf_op jit(solution)/shard_map/ppermute | solution.py:278
  24.8 1.0 %copy-start.3 = (bf16[256,1024]{1,0:T(8,128)(2,1)S(1)}, bf16[256,1024]{1,0:T(8,128)(2,1)}, u32[]{:S(2)}) copy-start(bf16[256,1024]{1,0:T(8,128)(2,1)} %constant.27.clone.joined) | copy-start | bytes 1572868
  25.8 5.1 %copy-start.4 = (bf16[256,1024]{1,0:T(8,128)(2,1)S(1)}, bf16[256,1024]{1,0:T(8,128)(2,1)}, u32[]{:S(2)}) copy-start(bf16[256,1024]{1,0:T(8,128)(2,1)} %constant.27.clone.joined) | copy-start | bytes 1572868
  55.9 12.3 %collective-permute-start.2 = (f32[24,128]{1,0:T(8,128)S(1)}, f32[24,128]{1,0:T(8,128)S(1)}, u32[]{:S(2)}, u32[]{:S(2)}) collective-permute-start(f32[24,128]{1,0:T(8,128)S(1)} %slice.9), channel_id=1, source_target_pairs={{0,64},{32,96},{64,128},{96,160},{128,192},{160,224},{192,256},{22... | collective-permute-start | bytes 36872 | tf_op jit(solution)/shard_map/ppermute | solution.py:287

commit v4 on v3

--- a/solution.py
+++ b/solution.py
@@ -126,11 +126,9 @@
     return gather_rows(field[:, : 2 * Z] + jnp.where(both, field[:, 2 * Z :], 0.0))
 
 
-def own_kernel(
-    odd_ref, t_ref, p_ref, q_ref, joined, kernel, o_ref, pairs, work
-):
+def own_kernel(flags_ref, t_ref, p_ref, q_ref, joined, kernel, o_ref, pairs, work):
     z4, x8, y_in, y_out = views(joined)
-    odd = odd_ref[0] == 1
+    odd = flags_ref[0] == 1
     high = XB * HALF
     for step in range(GROUPS):
         rows, rows2 = chunk(step, high), chunk(step, high, X * HALF)
@@ -149,11 +147,10 @@
         o_ref[pl.ds(step * XB, XB)] = outward(work, step, partner, odd, z4, y_out)
 
 
-def cross_kernel(
-    odd_ref, t_ref, pairs, own_ref, joined, kernel, o_ref, work
-):
+def cross_kernel(flags_ref, t_ref, pairs, own_ref, joined, kernel, o_ref, work):
     z4, x8, y_in, y_out = views(joined)
-    even = odd_ref[0] == 0
+    even = flags_ref[0] == 0
+    border = flags_ref[1] == 1
     for step in range(GROUPS):
         partner = pairs[chunk(step, ROWS), :]
         field = density(t_ref[chunk(step, XB * HALF), :], partner)
@@ -162,31 +159,14 @@
     for step in range(GROUPS):
         partner = pairs[chunk(step, ROWS), :]
         cross = outward(work, step, partner, even, z4, y_out)
+        turned = jnp.concatenate([cross[i : i + 1] for i in reversed(range(XB))], axis=0)
+        cross = jnp.where(border, turned, cross)
         planes = pl.ds(step * XB, XB)
         o_ref[planes] = jnp.concatenate([own_ref[planes], cross], axis=1).astype(bf16)
 
 
 def rows_kernel(x_ref, o_ref):
     o_ref[...] = x_ref[...].reshape(o_ref.shape)
-
-
-PARTS = 4
-
-
-def split_rows_kernel(x_ref, o_ref, landed, sems):
-    width = x_ref.shape[1] // PARTS
-    high = o_ref.shape[0] // PARTS
-    copies = []
-    for part in range(PARTS):
-        columns = slice(part * width, (part + 1) * width)
-        copies.append(
-            pltpu.make_async_copy(x_ref.at[:, columns], landed.at[:, columns], sems.at[part])
-        )
-        copies[-1].start()
-    for part, copy in enumerate(copies):
-        copy.wait()
-        field = landed[:, part * width : (part + 1) * width]
-        o_ref[part * high : (part + 1) * high, :] = field.reshape(high, 2 * Z)
 
 
 VMEM = pl.BlockSpec(memory_space=pltpu.VMEM)
@@ -206,24 +186,11 @@
     )(fields)
 
 
-def as_rows_early(fields):
-    return pl.pallas_call(
-        split_rows_kernel,
-        out_shape=jax.ShapeDtypeStruct((fields.shape[0] * X * HALF, 2 * Z), bf16),
-        in_specs=[pl.BlockSpec(memory_space=pltpu.HBM)],
-        out_specs=VMEM,
-        scratch_shapes=[pltpu.VMEM(fields.shape, bf16), pltpu.SemaphoreType.DMA((PARTS,))],
-        cost_estimate=pl.CostEstimate(flops=0, bytes_accessed=10**6, transcendentals=0),
-        compiler_params=GRANT,
-        name="as_rows_early",
-    )(fields)
-
-
 COST = pl.CostEstimate(flops=4 * 10**9, bytes_accessed=3 * 10**6, transcendentals=0)
 WORK = pltpu.VMEM((X, Y, 4 * Z), f32)
 
 
-def own_call(odd, trial, partner, other, tabs):
+def own_call(flags, trial, partner, other, tabs):
     return pl.pallas_call(
         own_kernel,
         out_shape=(
@@ -236,10 +203,10 @@
         cost_estimate=COST,
         compiler_params=GRANT,
         name="own_terms",
-    )(odd, trial, partner, other, *tabs)
-
-
-def cross_call(odd, trial, pairs, own, tabs):
+    )(flags, trial, partner, other, *tabs)
+
+
+def cross_call(flags, trial, pairs, own, tabs):
     return pl.pallas_call(
         cross_kernel,
         out_shape=jax.ShapeDtypeStruct((X, Y, 2 * Z), bf16),
@@ -249,7 +216,7 @@
         cost_estimate=COST,
         compiler_params=GRANT,
         name="cross_terms",
-    )(odd, trial, pairs, own, *tabs)
+    )(flags, trial, pairs, own, *tabs)
 
 
 LOW = 4
@@ -271,20 +238,33 @@
     return pairs
 
 
+def slab_route(blocks, groups):
+    half = blocks // 2
+    pairs = []
+    for block in range(blocks):
+        owner = (block + 2) % blocks
+        for group in range(groups):
+            mirror = group // LOW * LOW + LOW - 1 - group % LOW
+            place = mirror if owner // half != block // half else group
+            pairs.append((block * groups + group, owner * groups + place))
+    return pairs
+
+
 def local(targets, partners):
     blocks, groups = lax.axis_size("orb"), lax.axis_size("grp")
     block = lax.axis_index("orb")
-    target = as_rows_early(targets)
+    target = as_rows(targets)
     remote = lax.ppermute(target, ("orb", "grp"), trial_route(blocks, groups))
     partner = as_rows(partners)
     other = lax.ppermute(partner, "orb", [(i ^ 1, i) for i in range(blocks)])
     tabs = tables()
-    odd = (block % 2).astype(jnp.int32).reshape(1)
-    own, pairs = own_call(odd, target, partner, other, tabs)
-    fields = cross_call(odd, remote, pairs, own, tabs)
+    half = blocks // 2
+    flags = jnp.stack([block % 2, (block % half >= half - 2).astype(jnp.int32)])
+    own, pairs = own_call(flags, target, partner, other, tabs)
+    fields = cross_call(flags, remote, pairs, own, tabs)
     slabs = lax.all_to_all(fields, "grp", 0, 0, tiled=True)
     summed = jnp.sum(slabs.astype(f32), axis=0)
-    ahead = lax.ppermute(summed[HALF:], "orb", [(i, (i + 2) % blocks) for i in range(blocks)])
+    ahead = lax.ppermute(summed[HALF:], ("orb", "grp"), slab_route(blocks, groups))
     factor = -1.0 / math.sqrt(STEPS * groups * 2)
     return ((summed[:HALF] + ahead) * factor).reshape(1, Y * Z)
 

time: 69.1 us -> 67.2 us (0.973)
  waiting for transfers between devices: 13 us -> 10.5 us
    ppermute x1, waiting for transfers between devices: 10.3 us -> 8.43 us  [local(): lax.ppermute(summed[HALF:], ('orb', 'grp'), slab_route(blocks, groups))]
where the time goes in v4:
time: 67.2 us; the launch traced here: 66.9 us
  starting transfers between devices  25 us (37%)
  blocking collectives  22.7 us (34%)
  waiting for transfers between devices  10.5 us (16%)
  Pallas kernels  5.86 us (9%)
  local copies, waits for them, and re-layouts  2.06 us (3%)
  other arithmetic  0.75 us (1%)
    all_to_all x1, blocking collectives, local(): slabs = lax.all_to_all(fields, 'grp', 0, 0, tiled=True)  22.7 us
    ppermute x1, starting transfers between devices, local(): remote = lax.ppermute(target, ('orb', 'grp'), trial_route(blocks, groups))  21 us
    ppermute x1, waiting for transfers between devices, local(): lax.ppermute(summed[HALF:], ('orb', 'grp'), slab_route(blocks, groups))  8.43 us
    pallas_call x1, Pallas kernels, own_call(): pl.pallas_call(own_kernel, out_shape=(jax.ShapeDtypeStruct((X, HALF, 2 *...  2.9 us
    pallas_call x1, Pallas kernels, cross_call(): pl.pallas_call(cross_kernel, out_shape=jax.ShapeDtypeStruct((X, Y, 2 * Z)...  2.87 us
    ppermute x1, waiting for transfers between devices, local(): remote = lax.ppermute(target, ('orb', 'grp'), trial_route(blocks, groups))  2.08 us
    ppermute x1, starting transfers between devices, local(): other = lax.ppermute(partner, 'orb', [(i ^ 1, i) for i in range(blocks)])  2.05 us
    unnamed x10, local copies, waits for them, and re-layouts  2.05 us
  transfers between devices with their start and end apart: 3, of which 2 were waited for; matrix products, arithmetic and copies ran while one was open for 0% of the time, Pallas kernels for 4%

profile of v4, /device:TPU:2, one launch (start us, length us, event | category | flops | bytes accessed | tf_op | source)
XLA Modules:
  0.0 66.9 jit_solution(2655009651510891621)
XLA Ops:
  0.0 0.0 copy-start
  0.0 1.0 %copy-done = bf16[2,98304]{1,0:T(2,128)(2,1)S(1)} copy-done((bf16[2,98304]{1,0:T(2,128)(2,1)S(1)}, bf16[2,98304]{1,0:T(2,128)(2,1)}, u32[]{:S(2)}) %copy-start) | copy-done | bytes 393240
  1.0 0.0 copy-start.1
  1.0 0.0 copy-start.2
  1.0 0.1 as_rows.3.p_ref
  1.1 2.1 %collective-permute-start.1 = (bf16[1536,128]{1,0:T(8,128)(2,1)S(1)}, bf16[1536,128]{1,0:T(8,128)(2,1)S(1)}, u32[]{:S(2)}, u32[]{:S(2)}) collective-permute-start(bf16[1536,128]{1,0:T(8,128)(2,1)S(1)} %as_rows.3.p_ref), channel_id=1, source_target_pairs={{32,0},{0,32},{96,64},{64,96},{160,128},{128,160},{224,192},{192,2... | collective-permute-start | bytes 1179656 | tf_op jit(solution)/shard_map/ppermute | solution.py:259
  3.1 0.0 copy-done.1
  3.2 21.0 %collective-permute-start = (bf16[768,128]{1,0:T(8,128)(2,1)S(1)}, bf16[768,128]{1,0:T(8,128)(2,1)S(1)}, u32[]{:S(2)}, u32[]{:S(2)}) collective-permute-start(bf16[768,128]{1,0:T(8,128)(2,1)S(1)} %as_rows.2.t_ref), channel_id=1, source_target_pairs={{64,0},{65,1},{66,2},{67,3},{68,4},{69,5},{70,6},{71,7},{72,8},{73... | collective-permute-start | bytes 589832 | tf_op jit(solution)/shard_map/ppermute | solution.py:257
  24.2 0.1 pad_add_fusion.flags_ref
  24.3 0.0 collective-permute-done.1.q_ref
  24.3 0.0 copy-done.2
  24.3 0.0 copy-start.3
  24.3 1.0 %copy-done.3 = bf16[256,1024]{1,0:T(8,128)(2,1)S(1)} copy-done((bf16[256,1024]{1,0:T(8,128)(2,1)S(1)}, bf16[256,1024]{1,0:T(8,128)(2,1)}, u32[]{:S(2)}) %copy-start.3) | copy-done | bytes 524312
  25.3 0.0 copy-start.4
  25.3 2.9 %own_terms.1 = (f32[32,24,128]{2,1,0:T(8,128)S(1)}, bf16[1536,256]{1,0:T(8,128)(2,1)S(1)}) custom-call(s32[2]{0:T(128)S(1)} %pad_add_fusion.flags_ref, bf16[768,128]{1,0:T(8,128)(2,1)S(1)} %as_rows.2.t_ref, bf16[1536,128]{1,0:T(8,128)(2,1)S(1)} %as_rows.3.p_ref, bf16[1536,128]{1,0:T(8,128)(2,1)S(1)} %collective-permute-done.1.q_ref, ...), custom_call_target="tpu_custom_call" | custom-call | flops 4000000000 | bytes 3000000 | tf_op jit(solution)/shard_map/own_terms/pallas_call | solution.py:194
  28.2 2.1 %collective-permute-done.t_ref = bf16[768,128]{1,0:T(8,128)(2,1)S(1)} collective-permute-done((bf16[768,128]{1,0:T(8,128)(2,1)S(1)}, bf16[768,128]{1,0:T(8,128)(2,1)S(1)}, u32[]{:S(2)}, u32[]{:S(2)}) %collective-permute-start) | collective-permute-done | bytes 196640 | tf_op jit(solution)/shard_map/ppermute | solution.py:257
  30.3 0.0 copy-done.4
  30.3 2.9 %cross_terms.1 = bf16[32,48,128]{2,1,0:T(8,128)(2,1)S(1)} custom-call(s32[2]{0:T(128)S(1)} %pad_add_fusion.flags_ref, bf16[768,128]{1,0:T(8,128)(2,1)S(1)} %collective-permute-done.t_ref, bf16[1536,256]{1,0:T(8,128)(2,1)S(1)} %get-tuple-element.7.pairs, f32[32,24,128]{2,1,0:T(8,128)S(1)} %get-tuple-element.8.own_ref, bf16[256,1024]{1,0:T(8,128)(2,1)S(1)} %copy-done.4, ...), custom_call_target="tpu_custom_call" | custom-call | flops 4000000000 | bytes 3000000 | tf_op jit(solution)/shard_map/cross_terms/pallas_call | solution.py:210
  33.2 22.7 %all_to_all.5 = bf16[32,48,128]{2,1,0:T(8,128)(2,1)S(1)} all-to-all(bf16[32,48,128]{2,1,0:T(8,128)(2,1)S(1)} %cross_terms.1), channel_id=1, replica_groups=mesh['orb'=32,'grp'=32] {'grp'}, dimensions={0} | all-to-all | bytes 786432 | tf_op jit(solution)/shard_map/all_to_all | solution.py:265
  55.9 0.1 convert_reduce_fusion
  55.9 1.9 %collective-permute-start.2 = (f32[24,128]{1,0:T(8,128)S(1)}, f32[24,128]{1,0:T(8,128)S(1)}, u32[]{:S(2)}, u32[]{:S(2)}) collective-permute-start(f32[24,128]{1,0:T(8,128)S(1)} %slice.9), channel_id=1, source_target_pairs={{0,64},{1,65},{2,66},{3,67},{4,68},{5,69},{6,70},{7,71},{8,72},{9,... | collective-permute-start | bytes 36872 | tf_op jit(solution)/shard_map/ppermute | solution.py:267
  57.9 8.4 %collective-permute-done.2 = f32[24,128]{1,0:T(8,128)S(1)} collective-permute-done((f32[24,128]{1,0:T(8,128)S(1)}, f32[24,128]{1,0:T(8,128)S(1)}, u32[]{:S(2)}, u32[]{:S(2)}) %collective-permute-start.2) | collective-permute-done | bytes 12320 | tf_op jit(solution)/shard_map/ppermute | solution.py:267
  66.3 0.6 fusion
  (2 shorter events, 0.0 us)
Async XLA Ops:
  0.0 1.0 %copy-start = (bf16[2,98304]{1,0:T(2,128)(2,1)S(1)}, bf16[2,98304]{1,0:T(2,128)(2,1)}, u32[]{:S(2)}) copy-start(bf16[2,98304]{1,0:T(2,128)(2,1)} %x_ref.3) | copy-start | bytes 1179652
  1.0 2.1 %copy-start.1 = (bf16[1,98304]{1,0:T(2,128)(2,1)S(1)}, bf16[1,98304]{1,0:T(2,128)(2,1)}, u32[]{:S(2)}) copy-start(bf16[1,98304]{1,0:T(2,128)(2,1)} %x_ref.2) | copy-start | bytes 589828
  1.0 23.3 %copy-start.2 = (f32[32,48,128]{2,1,0:T(8,128)S(1)}, f32[32,48,128]{2,1,0:T(8,128)}, u32[]{:S(2)}) copy-start(f32[32,48,128]{2,1,0:T(8,128)} %constant.38.clone.kernel) | copy-start | bytes 2359300
  1.1 23.2 %collective-permute-start.1 = (bf16[1536,128]{1,0:T(8,128)(2,1)S(1)}, bf16[1536,128]{1,0:T(8,128)(2,1)S(1)}, u32[]{:S(2)}, u32[]{:S(2)}) collective-permute-start(bf16[1536,128]{1,0:T(8,128)(2,1)S(1)} %as_rows.3.p_ref), channel_id=1, source_target_pairs={{32,0},{0,32},{96,64},{64,96},{160,128},{128,160},{224,192},{192,2... | collective-permute-start | bytes 1179656 | tf_op jit(solution)/shard_map/ppermute | solution.py:259
  3.2 27.2 %collective-permute-start = (bf16[768,128]{1,0:T(8,128)(2,1)S(1)}, bf16[768,128]{1,0:T(8,128)(2,1)S(1)}, u32[]{:S(2)}, u32[]{:S(2)}) collective-permute-start(bf16[768,128]{1,0:T(8,128)(2,1)S(1)} %as_rows.2.t_ref), channel_id=1, source_target_pairs={{64,0},{65,1},{66,2},{67,3},{68,4},{69,5},{70,6},{71,7},{72,8},{73... | collective-permute-start | bytes 589832 | tf_op jit(solution)/shard_map/ppermute | solution.py:257
  24.3 1.0 %copy-start.3 = (bf16[256,1024]{1,0:T(8,128)(2,1)S(1)}, bf16[256,1024]{1,0:T(8,128)(2,1)}, u32[]{:S(2)}) copy-start(bf16[256,1024]{1,0:T(8,128)(2,1)} %constant.39.clone.joined) | copy-start | bytes 1572868
  25.3 5.0 %copy-start.4 = (bf16[256,1024]{1,0:T(8,128)(2,1)S(1)}, bf16[256,1024]{1,0:T(8,128)(2,1)}, u32[]{:S(2)}) copy-start(bf16[256,1024]{1,0:T(8,128)(2,1)} %constant.39.clone.joined) | copy-start | bytes 1572868
  55.9 10.4 %collective-permute-start.2 = (f32[24,128]{1,0:T(8,128)S(1)}, f32[24,128]{1,0:T(8,128)S(1)}, u32[]{:S(2)}, u32[]{:S(2)}) collective-permute-start(f32[24,128]{1,0:T(8,128)S(1)} %slice.9), channel_id=1, source_target_pairs={{0,64},{1,65},{2,66},{3,67},{4,68},{5,69},{6,70},{7,71},{8,72},{9,... | collective-permute-start | bytes 36872 | tf_op jit(solution)/shard_map/ppermute | solution.py:267

commit v5 on v4

--- a/solution.py
+++ b/solution.py
@@ -126,9 +126,9 @@
     return gather_rows(field[:, : 2 * Z] + jnp.where(both, field[:, 2 * Z :], 0.0))
 
 
-def own_kernel(flags_ref, t_ref, p_ref, q_ref, joined, kernel, o_ref, pairs, work):
+def own_kernel(t_ref, p_ref, q_ref, joined, kernel, o_ref, pairs, work):
     z4, x8, y_in, y_out = views(joined)
-    odd = flags_ref[0] == 1
+    odd = lax.axis_index("orb") % 2 == 1
     high = XB * HALF
     for step in range(GROUPS):
         rows, rows2 = chunk(step, high), chunk(step, high, X * HALF)
@@ -147,10 +147,12 @@
         o_ref[pl.ds(step * XB, XB)] = outward(work, step, partner, odd, z4, y_out)
 
 
-def cross_kernel(flags_ref, t_ref, pairs, own_ref, joined, kernel, o_ref, work):
+def cross_kernel(t_ref, pairs, own_ref, joined, kernel, o_ref, work):
     z4, x8, y_in, y_out = views(joined)
-    even = flags_ref[0] == 0
-    border = flags_ref[1] == 1
+    block = lax.axis_index("orb")
+    half = lax.axis_size("orb") // 2
+    even = block % 2 == 0
+    border = block % half >= half - 2
     for step in range(GROUPS):
         partner = pairs[chunk(step, ROWS), :]
         field = density(t_ref[chunk(step, XB * HALF), :], partner)
@@ -170,7 +172,6 @@
 
 
 VMEM = pl.BlockSpec(memory_space=pltpu.VMEM)
-SMEM = pl.BlockSpec(memory_space=pltpu.SMEM)
 GRANT = pltpu.CompilerParams(vmem_limit_bytes=16 * 2**20)
 
 
@@ -190,33 +191,33 @@
 WORK = pltpu.VMEM((X, Y, 4 * Z), f32)
 
 
-def own_call(flags, trial, partner, other, tabs):
+def own_call(trial, partner, other, tabs):
     return pl.pallas_call(
         own_kernel,
         out_shape=(
             jax.ShapeDtypeStruct((X, HALF, 2 * Z), f32),
             jax.ShapeDtypeStruct((X * Y, 4 * Z), bf16),
         ),
-        in_specs=[SMEM] + [VMEM] * 5,
+        in_specs=[VMEM] * 5,
         out_specs=(VMEM, VMEM),
         scratch_shapes=[WORK],
         cost_estimate=COST,
         compiler_params=GRANT,
         name="own_terms",
-    )(flags, trial, partner, other, *tabs)
-
-
-def cross_call(flags, trial, pairs, own, tabs):
+    )(trial, partner, other, *tabs)
+
+
+def cross_call(trial, pairs, own, tabs):
     return pl.pallas_call(
         cross_kernel,
         out_shape=jax.ShapeDtypeStruct((X, Y, 2 * Z), bf16),
-        in_specs=[SMEM] + [VMEM] * 5,
+        in_specs=[VMEM] * 5,
         out_specs=VMEM,
         scratch_shapes=[WORK],
         cost_estimate=COST,
         compiler_params=GRANT,
         name="cross_terms",
-    )(flags, trial, pairs, own, *tabs)
+    )(trial, pairs, own, *tabs)
 
 
 LOW = 4
@@ -252,16 +253,13 @@
 
 def local(targets, partners):
     blocks, groups = lax.axis_size("orb"), lax.axis_size("grp")
-    block = lax.axis_index("orb")
+    tabs = tables()
     target = as_rows(targets)
     remote = lax.ppermute(target, ("orb", "grp"), trial_route(blocks, groups))
     partner = as_rows(partners)
     other = lax.ppermute(partner, "orb", [(i ^ 1, i) for i in range(blocks)])
-    tabs = tables()
-    half = blocks // 2
-    flags = jnp.stack([block % 2, (block % half >= half - 2).astype(jnp.int32)])
-    own, pairs = own_call(flags, target, partner, other, tabs)
-    fields = cross_call(flags, remote, pairs, own, tabs)
+    own, pairs = own_call(target, partner, other, tabs)
+    fields = cross_call(remote, pairs, own, tabs)
     slabs = lax.all_to_all(fields, "grp", 0, 0, tiled=True)
     summed = jnp.sum(slabs.astype(f32), axis=0)
     ahead = lax.ppermute(summed[HALF:], ("orb", "grp"), slab_route(blocks, groups))

time: 67.2 us -> 66.7 us (level)
  Pallas kernels: 5.86 us -> 4.75 us
    unnamed x10 -> x8, local copies, waits for them, and re-layouts: 2.05 us -> 2.04 us
where the time goes in v5:
time: 66.7 us; the launch traced here: 66.3 us
  starting transfers between devices  25 us (37%)
  blocking collectives  22.7 us (34%)
  waiting for transfers between devices  11.1 us (17%)
  Pallas kernels  4.75 us (7%)
  local copies, waits for them, and re-layouts  2.05 us (3%)
  other arithmetic  0.67 us (1%)
    all_to_all x1, blocking collectives, local(): slabs = lax.all_to_all(fields, 'grp', 0, 0, tiled=True)  22.7 us
    ppermute x1, starting transfers between devices, local(): remote = lax.ppermute(target, ('orb', 'grp'), trial_route(blocks, groups))  21 us
    ppermute x1, waiting for transfers between devices, local(): lax.ppermute(summed[HALF:], ('orb', 'grp'), slab_route(blocks, groups))  8.43 us
    ppermute x1, waiting for transfers between devices, local(): remote = lax.ppermute(target, ('orb', 'grp'), trial_route(blocks, groups))  2.71 us
    pallas_call x1, Pallas kernels, own_call(): pl.pallas_call(own_kernel, out_shape=(jax.ShapeDtypeStruct((X, HALF, 2 *...  2.35 us
    pallas_call x1, Pallas kernels, cross_call(): pl.pallas_call(cross_kernel, out_shape=jax.ShapeDtypeStruct((X, Y, 2 * Z)...  2.31 us
    ppermute x1, starting transfers between devices, local(): other = lax.ppermute(partner, 'orb', [(i ^ 1, i) for i in range(blocks)])  2.05 us
    unnamed x8, local copies, waits for them, and re-layouts  2.04 us
  transfers between devices with their start and end apart: 3, of which 2 were waited for; matrix products, arithmetic and copies ran while one was open for 0% of the time, Pallas kernels for 4%

profile of v5, /device:TPU:2, one launch (start us, length us, event | category | flops | bytes accessed | tf_op | source)
XLA Modules:
  0.0 66.3 jit_solution(14893021042250761247)
XLA Ops:
  0.0 0.0 copy-start
  0.0 1.0 %copy-done = bf16[2,98304]{1,0:T(2,128)(2,1)S(1)} copy-done((bf16[2,98304]{1,0:T(2,128)(2,1)S(1)}, bf16[2,98304]{1,0:T(2,128)(2,1)}, u32[]{:S(2)}) %copy-start) | copy-done | bytes 393240
  1.0 0.0 copy-start.1
  1.0 0.0 copy-start.2
  1.0 0.1 as_rows.3.p_ref
  1.1 2.1 %collective-permute-start.1 = (bf16[1536,128]{1,0:T(8,128)(2,1)S(1)}, bf16[1536,128]{1,0:T(8,128)(2,1)S(1)}, u32[]{:S(2)}, u32[]{:S(2)}) collective-permute-start(bf16[1536,128]{1,0:T(8,128)(2,1)S(1)} %as_rows.3.p_ref), channel_id=1, source_target_pairs={{32,0},{0,32},{96,64},{64,96},{160,128},{128,160},{224,192},{192,2... | collective-permute-start | bytes 1179656 | tf_op jit(solution)/shard_map/ppermute | solution.py:260
  3.1 0.0 copy-done.1
  3.2 21.0 %collective-permute-start = (bf16[768,128]{1,0:T(8,128)(2,1)S(1)}, bf16[768,128]{1,0:T(8,128)(2,1)S(1)}, u32[]{:S(2)}, u32[]{:S(2)}) collective-permute-start(bf16[768,128]{1,0:T(8,128)(2,1)S(1)} %as_rows.2.t_ref), channel_id=1, source_target_pairs={{64,0},{65,1},{66,2},{67,3},{68,4},{69,5},{70,6},{71,7},{72,8},{73... | collective-permute-start | bytes 589832 | tf_op jit(solution)/shard_map/ppermute | solution.py:258
  24.2 0.0 collective-permute-done.1.q_ref
  24.2 0.0 copy-done.2
  24.2 0.0 copy-start.3
  24.2 1.0 %copy-done.3 = bf16[256,1024]{1,0:T(8,128)(2,1)S(1)} copy-done((bf16[256,1024]{1,0:T(8,128)(2,1)S(1)}, bf16[256,1024]{1,0:T(8,128)(2,1)}, u32[]{:S(2)}) %copy-start.3) | copy-done | bytes 524312
  25.3 2.3 %own_terms.1 = (f32[32,24,128]{2,1,0:T(8,128)S(1)}, bf16[1536,256]{1,0:T(8,128)(2,1)S(1)}) custom-call(bf16[768,128]{1,0:T(8,128)(2,1)S(1)} %as_rows.2.t_ref, bf16[1536,128]{1,0:T(8,128)(2,1)S(1)} %as_rows.3.p_ref, bf16[1536,128]{1,0:T(8,128)(2,1)S(1)} %collective-permute-done.1.q_ref, bf16[256,1024]{1,0:T(8,128)(2,1)S(1)} %copy-done.3, ...), custom_call_target="tpu_custom_call" | custom-call | flops 4000000000 | bytes 3000000 | tf_op jit(solution)/shard_map/own_terms/pallas_call | solution.py:195
  27.6 2.7 %collective-permute-done.t_ref = bf16[768,128]{1,0:T(8,128)(2,1)S(1)} collective-permute-done((bf16[768,128]{1,0:T(8,128)(2,1)S(1)}, bf16[768,128]{1,0:T(8,128)(2,1)S(1)}, u32[]{:S(2)}, u32[]{:S(2)}) %collective-permute-start) | collective-permute-done | bytes 196640 | tf_op jit(solution)/shard_map/ppermute | solution.py:258
  30.3 2.3 %cross_terms.1 = bf16[32,48,128]{2,1,0:T(8,128)(2,1)S(1)} custom-call(bf16[768,128]{1,0:T(8,128)(2,1)S(1)} %collective-permute-done.t_ref, bf16[1536,256]{1,0:T(8,128)(2,1)S(1)} %get-tuple-element.7.pairs, f32[32,24,128]{2,1,0:T(8,128)S(1)} %get-tuple-element.8.own_ref, bf16[256,1024]{1,0:T(8,128)(2,1)S(1)} %copy-done.3, f32[32,48,128]{2,1,0:T(8,128)S(1)} %copy-done.2), custom_call_target="tpu_custom_call" | custom-call | flops 4000000000 | bytes 3000000 | tf_op jit(solution)/shard_map/cross_terms/pallas_call | solution.py:211
  32.6 22.7 %all_to_all.5 = bf16[32,48,128]{2,1,0:T(8,128)(2,1)S(1)} all-to-all(bf16[32,48,128]{2,1,0:T(8,128)(2,1)S(1)} %cross_terms.1), channel_id=1, replica_groups=mesh['orb'=32,'grp'=32] {'grp'}, dimensions={0} | all-to-all | bytes 786432 | tf_op jit(solution)/shard_map/all_to_all | solution.py:263
  55.3 0.1 convert_reduce_fusion
  55.4 1.9 %collective-permute-start.2 = (f32[24,128]{1,0:T(8,128)S(1)}, f32[24,128]{1,0:T(8,128)S(1)}, u32[]{:S(2)}, u32[]{:S(2)}) collective-permute-start(f32[24,128]{1,0:T(8,128)S(1)} %slice.9), channel_id=1, source_target_pairs={{0,64},{1,65},{2,66},{3,67},{4,68},{5,69},{6,70},{7,71},{8,72},{9,... | collective-permute-start | bytes 36872 | tf_op jit(solution)/shard_map/ppermute | solution.py:265
  57.3 8.4 %collective-permute-done.2 = f32[24,128]{1,0:T(8,128)S(1)} collective-permute-done((f32[24,128]{1,0:T(8,128)S(1)}, f32[24,128]{1,0:T(8,128)S(1)}, u32[]{:S(2)}, u32[]{:S(2)}) %collective-permute-start.2) | collective-permute-done | bytes 12320 | tf_op jit(solution)/shard_map/ppermute | solution.py:265
  65.7 0.6 fusion
  (2 shorter events, 0.0 us)
Async XLA Ops:
  0.0 1.0 %copy-start = (bf16[2,98304]{1,0:T(2,128)(2,1)S(1)}, bf16[2,98304]{1,0:T(2,128)(2,1)}, u32[]{:S(2)}) copy-start(bf16[2,98304]{1,0:T(2,128)(2,1)} %x_ref.3) | copy-start | bytes 1179652
  1.0 2.1 %copy-start.1 = (bf16[1,98304]{1,0:T(2,128)(2,1)S(1)}, bf16[1,98304]{1,0:T(2,128)(2,1)}, u32[]{:S(2)}) copy-start(bf16[1,98304]{1,0:T(2,128)(2,1)} %x_ref.2) | copy-start | bytes 589828
  1.0 23.2 %copy-start.2 = (f32[32,48,128]{2,1,0:T(8,128)S(1)}, f32[32,48,128]{2,1,0:T(8,128)}, u32[]{:S(2)}) copy-start(f32[32,48,128]{2,1,0:T(8,128)} %constant.8.clone.kernel) | copy-start | bytes 2359300
  1.1 23.1 %collective-permute-start.1 = (bf16[1536,128]{1,0:T(8,128)(2,1)S(1)}, bf16[1536,128]{1,0:T(8,128)(2,1)S(1)}, u32[]{:S(2)}, u32[]{:S(2)}) collective-permute-start(bf16[1536,128]{1,0:T(8,128)(2,1)S(1)} %as_rows.3.p_ref), channel_id=1, source_target_pairs={{32,0},{0,32},{96,64},{64,96},{160,128},{128,160},{224,192},{192,2... | collective-permute-start | bytes 1179656 | tf_op jit(solution)/shard_map/ppermute | solution.py:260
  3.2 27.2 %collective-permute-start = (bf16[768,128]{1,0:T(8,128)(2,1)S(1)}, bf16[768,128]{1,0:T(8,128)(2,1)S(1)}, u32[]{:S(2)}, u32[]{:S(2)}) collective-permute-start(bf16[768,128]{1,0:T(8,128)(2,1)S(1)} %as_rows.2.t_ref), channel_id=1, source_target_pairs={{64,0},{65,1},{66,2},{67,3},{68,4},{69,5},{70,6},{71,7},{72,8},{73... | collective-permute-start | bytes 589832 | tf_op jit(solution)/shard_map/ppermute | solution.py:258
  24.2 1.0 %copy-start.3 = (bf16[256,1024]{1,0:T(8,128)(2,1)S(1)}, bf16[256,1024]{1,0:T(8,128)(2,1)}, u32[]{:S(2)}) copy-start(bf16[256,1024]{1,0:T(8,128)(2,1)} %constant.9.clone.joined) | copy-start | bytes 1572868
  55.4 10.4 %collective-permute-start.2 = (f32[24,128]{1,0:T(8,128)S(1)}, f32[24,128]{1,0:T(8,128)S(1)}, u32[]{:S(2)}, u32[]{:S(2)}) collective-permute-start(f32[24,128]{1,0:T(8,128)S(1)} %slice.9), channel_id=1, source_target_pairs={{0,64},{1,65},{2,66},{3,67},{4,68},{5,69},{6,70},{7,71},{8,72},{9,... | collective-permute-start | bytes 36872 | tf_op jit(solution)/shard_map/ppermute | solution.py:265

commit v6 on v5

--- a/solution.py
+++ b/solution.py
@@ -147,24 +147,32 @@
         o_ref[pl.ds(step * XB, XB)] = outward(work, step, partner, odd, z4, y_out)
 
 
-def cross_kernel(t_ref, pairs, own_ref, joined, kernel, o_ref, work):
+def cross_kernel(r_ref, t_ref, c_ref, pairs, own_ref, joined, kernel, o_ref, work, first):
     z4, x8, y_in, y_out = views(joined)
     block = lax.axis_index("orb")
     half = lax.axis_size("orb") // 2
     even = block % 2 == 0
     border = block % half >= half - 2
-    for step in range(GROUPS):
-        partner = pairs[chunk(step, ROWS), :]
-        field = density(t_ref[chunk(step, XB * HALF), :], partner)
-        work[pl.ds(step * XB, XB)] = inward(field, z4, y_in)
+    high = XB * HALF
+    for step in range(GROUPS):
+        rows, rows2 = chunk(step, high), chunk(step, high, X * HALF)
+        trial = jnp.where(even, r_ref[rows, :].astype(f32), t_ref[rows, :].astype(f32))
+        kept = pairs[chunk(step, ROWS), :]
+        carried = spread_rows(c_ref[rows, :], c_ref[rows2, :])
+        partner = jnp.where(even, kept[:, : 2 * Z].astype(f32), carried.astype(f32)).astype(bf16)
+        first[chunk(step, ROWS), :] = partner
+        partner = jnp.concatenate([partner, kept[:, 2 * Z :]], axis=1)
+        work[pl.ds(step * XB, XB)] = inward(density(trial, partner), z4, y_in)
     middle(work, x8, kernel, 4 * Z)
     for step in range(GROUPS):
-        partner = pairs[chunk(step, ROWS), :]
+        rows = chunk(step, ROWS)
+        partner = jnp.concatenate([first[rows, :], pairs[rows, 2 * Z :]], axis=1)
         cross = outward(work, step, partner, even, z4, y_out)
+        planes = pl.ds(step * XB, XB)
+        own = own_ref[planes] + jnp.where(even, 0.0, cross)
         turned = jnp.concatenate([cross[i : i + 1] for i in reversed(range(XB))], axis=0)
         cross = jnp.where(border, turned, cross)
-        planes = pl.ds(step * XB, XB)
-        o_ref[planes] = jnp.concatenate([own_ref[planes], cross], axis=1).astype(bf16)
+        o_ref[planes] = jnp.concatenate([own, cross], axis=1).astype(bf16)
 
 
 def rows_kernel(x_ref, o_ref):
@@ -207,62 +215,50 @@
     )(trial, partner, other, *tabs)
 
 
-def cross_call(trial, pairs, own, tabs):
+def cross_call(remote, trial, carried, pairs, own, tabs):
     return pl.pallas_call(
         cross_kernel,
         out_shape=jax.ShapeDtypeStruct((X, Y, 2 * Z), bf16),
-        in_specs=[VMEM] * 5,
+        in_specs=[VMEM] * 7,
         out_specs=VMEM,
-        scratch_shapes=[WORK],
+        scratch_shapes=[WORK, pltpu.VMEM((X * Y, 2 * Z), bf16)],
         cost_estimate=COST,
         compiler_params=GRANT,
         name="cross_terms",
-    )(trial, pairs, own, *tabs)
+    )(remote, trial, carried, pairs, own, *tabs)
 
 
 LOW = 4
 
 
-def trial_route(blocks, groups):
+def route(blocks, groups, distance, parity):
     half = blocks // 2
     pairs = []
-    for block in range(blocks):
-        source = (block + 2) % blocks
-        for group in range(groups):
-            place = group % LOW
-            if source // half != block // half:
-                if block % 2 == 0:
-                    place = LOW - 1 - place
-                else:
-                    place = (place + (1 if block >= half else LOW - 1)) % LOW
-            pairs.append((source * groups + group // LOW * LOW + place, block * groups + group))
-    return pairs
-
-
-def slab_route(blocks, groups):
-    half = blocks // 2
-    pairs = []
-    for block in range(blocks):
-        owner = (block + 2) % blocks
+    for block in range(parity, blocks, 2):
+        target = (block + distance) % blocks
         for group in range(groups):
             mirror = group // LOW * LOW + LOW - 1 - group % LOW
-            place = mirror if owner // half != block // half else group
-            pairs.append((block * groups + group, owner * groups + place))
+            place = mirror if target // half != block // half else group
+            pairs.append((block * groups + group, target * groups + place))
     return pairs
 
 
 def local(targets, partners):
     blocks, groups = lax.axis_size("orb"), lax.axis_size("grp")
+    send = lambda what, distance, parity: lax.ppermute(
+        what, ("orb", "grp"), route(blocks, groups, distance, parity)
+    )
     tabs = tables()
     target = as_rows(targets)
-    remote = lax.ppermute(target, ("orb", "grp"), trial_route(blocks, groups))
+    remote = send(target, -2, 0)
     partner = as_rows(partners)
+    carried = send(partner, 2, 1)
     other = lax.ppermute(partner, "orb", [(i ^ 1, i) for i in range(blocks)])
     own, pairs = own_call(target, partner, other, tabs)
-    fields = cross_call(remote, pairs, own, tabs)
+    fields = cross_call(remote, target, carried, pairs, own, tabs)
     slabs = lax.all_to_all(fields, "grp", 0, 0, tiled=True)
     summed = jnp.sum(slabs.astype(f32), axis=0)
-    ahead = lax.ppermute(summed[HALF:], ("orb", "grp"), slab_route(blocks, groups))
+    ahead = send(summed[HALF:], 2, 0)
     factor = -1.0 / math.sqrt(STEPS * groups * 2)
     return ((summed[:HALF] + ahead) * factor).reshape(1, Y * Z)
 

time: 66.7 us -> 63.3 us (0.949)
  blocking collectives: 22.7 us -> 19.6 us
  waiting for transfers between devices: 11.1 us -> 10.1 us
  starting transfers between devices: 25 us -> 25.7 us
    all_to_all x1, blocking collectives: 22.7 us -> 19.6 us  [local(): slabs = lax.all_to_all(fields, 'grp', 0, 0, tiled=True)]
    ppermute x2 -> x3, waiting for transfers between devices: 11.1 us -> 10.1 us  [local(): lax.ppermute(what, ('orb', 'grp'), route(blocks, groups, distance, parity))]
    ppermute x2 -> x3, starting transfers between devices: 22.9 us -> 23.6 us  [local(): lax.ppermute(what, ('orb', 'grp'), route(blocks, groups, distance, parity))]
  transfers between devices with their start and end apart: 3 -> 4, of which waited for: 2 -> 1; matrix products, arithmetic and copies ran while one was open for 0% -> 0% of each run, Pallas kernels for 4% -> 4%
where the time goes in v6:
time: 63.3 us; the launch traced here: 63 us
  starting transfers between devices  25.7 us (41%)
  blocking collectives  19.6 us (31%)
  waiting for transfers between devices  10.1 us (16%)
  Pallas kernels  4.77 us (8%)
  local copies, waits for them, and re-layouts  2.05 us (3%)
  other arithmetic  0.67 us (1%)
    ppermute x3, starting transfers between devices, local(): lax.ppermute(what, ('orb', 'grp'), route(blocks, groups, distance, parity))  23.6 us
    all_to_all x1, blocking collectives, local(): slabs = lax.all_to_all(fields, 'grp', 0, 0, tiled=True)  19.6 us
    ppermute x3, waiting for transfers between devices, local(): lax.ppermute(what, ('orb', 'grp'), route(blocks, groups, distance, parity))  10.1 us
    pallas_call x1, Pallas kernels, own_call(): pl.pallas_call(own_kernel, out_shape=(jax.ShapeDtypeStruct((X, HALF, 2 *...  2.35 us
    pallas_call x1, Pallas kernels, cross_call(): pl.pallas_call(cross_kernel, out_shape=jax.ShapeDtypeStruct((X, Y, 2 * Z)...  2.33 us
    ppermute x1, starting transfers between devices, local(): other = lax.ppermute(partner, 'orb', [(i ^ 1, i) for i in range(blocks)])  2.05 us
    unnamed x8, local copies, waits for them, and re-layouts  2.04 us
  transfers between devices with their start and end apart: 4, of which 1 were waited for; matrix products, arithmetic and copies ran while one was open for 0% of the time, Pallas kernels for 4%

profile of v6, /device:TPU:2, one launch (start us, length us, event | category | flops | bytes accessed | tf_op | source)
XLA Modules:
  0.0 63.0 jit_solution(5195931777458477486)
XLA Ops:
  0.0 0.0 copy-start
  0.0 1.0 %copy-done = bf16[2,98304]{1,0:T(2,128)(2,1)S(1)} copy-done((bf16[2,98304]{1,0:T(2,128)(2,1)S(1)}, bf16[2,98304]{1,0:T(2,128)(2,1)}, u32[]{:S(2)}) %copy-start) | copy-done | bytes 393240
  1.0 0.0 copy-start.1
  1.0 0.0 copy-start.2
  1.0 0.1 as_rows.3.p_ref
  1.1 2.1 %collective-permute-start.2 = (bf16[1536,128]{1,0:T(8,128)(2,1)S(1)}, bf16[1536,128]{1,0:T(8,128)(2,1)S(1)}, u32[]{:S(2)}, u32[]{:S(2)}) collective-permute-start(bf16[1536,128]{1,0:T(8,128)(2,1)S(1)} %as_rows.3.p_ref), channel_id=1, source_target_pairs={{32,0},{0,32},{96,64},{64,96},{160,128},{128,160},{224,192},{192,2... | collective-permute-start | bytes 1179656 | tf_op jit(solution)/shard_map/ppermute | solution.py:256
  3.1 0.7 %collective-permute-start.1 = (bf16[1536,128]{1,0:T(8,128)(2,1)S(1)}, bf16[1536,128]{1,0:T(8,128)(2,1)S(1)}, u32[]{:S(2)}, u32[]{:S(2)}) collective-permute-start(bf16[1536,128]{1,0:T(8,128)(2,1)S(1)} %as_rows.3.p_ref), channel_id=1, source_target_pairs={{32,96},{33,97},{34,98},{35,99},{36,100},{37,101},{38,102},{39,103... | collective-permute-start | bytes 1179656 | tf_op jit(solution)/shard_map/ppermute | solution.py:248
  3.8 0.0 copy-done.1
  3.9 21.0 %collective-permute-start = (bf16[768,128]{1,0:T(8,128)(2,1)S(1)}, bf16[768,128]{1,0:T(8,128)(2,1)S(1)}, u32[]{:S(2)}, u32[]{:S(2)}) collective-permute-start(bf16[768,128]{1,0:T(8,128)(2,1)S(1)} %as_rows.2.t_ref), channel_id=1, source_target_pairs={{0,963},{1,962},{2,961},{3,960},{4,967},{5,966},{6,965},{7,964},{8... | collective-permute-start | bytes 589832 | tf_op jit(solution)/shard_map/ppermute | solution.py:248
  24.9 0.0 collective-permute-done.2.q_ref
  24.9 0.0 copy-done.2
  24.9 0.0 copy-start.3
  24.9 1.0 %copy-done.3 = bf16[256,1024]{1,0:T(8,128)(2,1)S(1)} copy-done((bf16[256,1024]{1,0:T(8,128)(2,1)S(1)}, bf16[256,1024]{1,0:T(8,128)(2,1)}, u32[]{:S(2)}) %copy-start.3) | copy-done | bytes 524312
  26.0 2.3 %own_terms.1 = (f32[32,24,128]{2,1,0:T(8,128)S(1)}, bf16[1536,256]{1,0:T(8,128)(2,1)S(1)}) custom-call(bf16[768,128]{1,0:T(8,128)(2,1)S(1)} %as_rows.2.t_ref, bf16[1536,128]{1,0:T(8,128)(2,1)S(1)} %as_rows.3.p_ref, bf16[1536,128]{1,0:T(8,128)(2,1)S(1)} %collective-permute-done.2.q_ref, bf16[256,1024]{1,0:T(8,128)(2,1)S(1)} %copy-done.3, ...), custom_call_target="tpu_custom_call" | custom-call | flops 4000000000 | bytes 3000000 | tf_op jit(solution)/shard_map/own_terms/pallas_call | solution.py:203
  28.3 0.0 collective-permute-done.r_ref
  28.3 0.0 collective-permute-done.1.c_ref
  28.3 2.3 %cross_terms.1 = bf16[32,48,128]{2,1,0:T(8,128)(2,1)S(1)} custom-call(bf16[768,128]{1,0:T(8,128)(2,1)S(1)} %collective-permute-done.r_ref, bf16[768,128]{1,0:T(8,128)(2,1)S(1)} %as_rows.2.t_ref, bf16[1536,128]{1,0:T(8,128)(2,1)S(1)} %collective-permute-done.1.c_ref, bf16[1536,256]{1,0:T(8,128)(2,1)S(1)} %get-tuple-element.7.pairs, ...), custom_call_target="tpu_custom_call" | custom-call | flops 4000000000 | bytes 3000000 | tf_op jit(solution)/shard_map/cross_terms/pallas_call | solution.py:219
  30.7 19.6 %all_to_all.5 = bf16[32,48,128]{2,1,0:T(8,128)(2,1)S(1)} all-to-all(bf16[32,48,128]{2,1,0:T(8,128)(2,1)S(1)} %cross_terms.1), channel_id=1, replica_groups=mesh['orb'=32,'grp'=32] {'grp'}, dimensions={0} | all-to-all | bytes 786432 | tf_op jit(solution)/shard_map/all_to_all | solution.py:259
  50.3 0.1 convert_reduce_fusion
  50.4 1.9 %collective-permute-start.3 = (f32[24,128]{1,0:T(8,128)S(1)}, f32[24,128]{1,0:T(8,128)S(1)}, u32[]{:S(2)}, u32[]{:S(2)}) collective-permute-start(f32[24,128]{1,0:T(8,128)S(1)} %slice.9), channel_id=1, source_target_pairs={{0,64},{1,65},{2,66},{3,67},{4,68},{5,69},{6,70},{7,71},{8,72},{9,... | collective-permute-start | bytes 36872 | tf_op jit(solution)/shard_map/ppermute | solution.py:248
  52.3 10.1 %collective-permute-done.3 = f32[24,128]{1,0:T(8,128)S(1)} collective-permute-done((f32[24,128]{1,0:T(8,128)S(1)}, f32[24,128]{1,0:T(8,128)S(1)}, u32[]{:S(2)}, u32[]{:S(2)}) %collective-permute-start.3) | collective-permute-done | bytes 12320 | tf_op jit(solution)/shard_map/ppermute | solution.py:248
  62.4 0.6 fusion
  (2 shorter events, 0.0 us)
Async XLA Ops:
  0.0 1.0 %copy-start = (bf16[2,98304]{1,0:T(2,128)(2,1)S(1)}, bf16[2,98304]{1,0:T(2,128)(2,1)}, u32[]{:S(2)}) copy-start(bf16[2,98304]{1,0:T(2,128)(2,1)} %x_ref.3) | copy-start | bytes 1179652
  1.0 2.8 %copy-start.1 = (bf16[1,98304]{1,0:T(2,128)(2,1)S(1)}, bf16[1,98304]{1,0:T(2,128)(2,1)}, u32[]{:S(2)}) copy-start(bf16[1,98304]{1,0:T(2,128)(2,1)} %x_ref.2) | copy-start | bytes 589828
  1.0 23.9 %copy-start.2 = (f32[32,48,128]{2,1,0:T(8,128)S(1)}, f32[32,48,128]{2,1,0:T(8,128)}, u32[]{:S(2)}) copy-start(f32[32,48,128]{2,1,0:T(8,128)} %constant.8.clone.kernel) | copy-start | bytes 2359300
  1.1 23.8 %collective-permute-start.2 = (bf16[1536,128]{1,0:T(8,128)(2,1)S(1)}, bf16[1536,128]{1,0:T(8,128)(2,1)S(1)}, u32[]{:S(2)}, u32[]{:S(2)}) collective-permute-start(bf16[1536,128]{1,0:T(8,128)(2,1)S(1)} %as_rows.3.p_ref), channel_id=1, source_target_pairs={{32,0},{0,32},{96,64},{64,96},{160,128},{128,160},{224,192},{192,2... | collective-permute-start | bytes 1179656 | tf_op jit(solution)/shard_map/ppermute | solution.py:256
  3.1 25.2 %collective-permute-start.1 = (bf16[1536,128]{1,0:T(8,128)(2,1)S(1)}, bf16[1536,128]{1,0:T(8,128)(2,1)S(1)}, u32[]{:S(2)}, u32[]{:S(2)}) collective-permute-start(bf16[1536,128]{1,0:T(8,128)(2,1)S(1)} %as_rows.3.p_ref), channel_id=1, source_target_pairs={{32,96},{33,97},{34,98},{35,99},{36,100},{37,101},{38,102},{39,103... | collective-permute-start | bytes 1179656 | tf_op jit(solution)/shard_map/ppermute | solution.py:248
  3.9 24.4 %collective-permute-start = (bf16[768,128]{1,0:T(8,128)(2,1)S(1)}, bf16[768,128]{1,0:T(8,128)(2,1)S(1)}, u32[]{:S(2)}, u32[]{:S(2)}) collective-permute-start(bf16[768,128]{1,0:T(8,128)(2,1)S(1)} %as_rows.2.t_ref), channel_id=1, source_target_pairs={{0,963},{1,962},{2,961},{3,960},{4,967},{5,966},{6,965},{7,964},{8... | collective-permute-start | bytes 589832 | tf_op jit(solution)/shard_map/ppermute | solution.py:248
  24.9 1.0 %copy-start.3 = (bf16[256,1024]{1,0:T(8,128)(2,1)S(1)}, bf16[256,1024]{1,0:T(8,128)(2,1)}, u32[]{:S(2)}) copy-start(bf16[256,1024]{1,0:T(8,128)(2,1)} %constant.9.clone.joined) | copy-start | bytes 1572868
  50.4 12.0 %collective-permute-start.3 = (f32[24,128]{1,0:T(8,128)S(1)}, f32[24,128]{1,0:T(8,128)S(1)}, u32[]{:S(2)}, u32[]{:S(2)}) collective-permute-start(f32[24,128]{1,0:T(8,128)S(1)} %slice.9), channel_id=1, source_target_pairs={{0,64},{1,65},{2,66},{3,67},{4,68},{5,69},{6,70},{7,71},{8,72},{9,... | collective-permute-start | bytes 36872 | tf_op jit(solution)/shard_map/ppermute | solution.py:248

commit v7 on v6

--- a/solution.py
+++ b/solution.py
@@ -111,43 +111,35 @@
     return pl.ds(pl.multiple_of(step * high + base, high), high)
 
 
-def density(trial, partner):
+def inward(trial, partner, z, y_in):
     trial = spread_rows(trial, trial)
-    return jnp.concatenate([trial * partner[:, : 2 * Z], trial * partner[:, 2 * Z :]], axis=1)
-
-
-def inward(field, z4, y_in):
-    return dot(y_in[...], dot(field, z4[...]).astype(bf16)).reshape(XB, Y, 4 * Z)
-
-
-def outward(work, step, partner, both, z4, y_out):
-    field = work[pl.ds(step * XB, XB)].reshape(ROWS, 4 * Z).astype(bf16)
-    field = dot(dot(y_out[...], field).astype(bf16), z4[...]) * partner.astype(f32)
-    return gather_rows(field[:, : 2 * Z] + jnp.where(both, field[:, 2 * Z :], 0.0))
-
-
-def own_kernel(t_ref, p_ref, q_ref, joined, kernel, o_ref, pairs, work):
+    parts = [trial * partner[:, at : at + 2 * Z] for at in range(0, partner.shape[1], 2 * Z)]
+    field = dot(jnp.concatenate(parts, axis=1), z).astype(bf16)
+    return dot(y_in[...], field).reshape(XB, Y, partner.shape[1])
+
+
+def outward(field, partner, z, y_out):
+    field = field.reshape(ROWS, partner.shape[1]).astype(bf16)
+    field = dot(dot(y_out[...], field).astype(bf16), z) * partner.astype(f32)
+    return gather_rows(sum(field[:, at : at + 2 * Z] for at in range(0, field.shape[1], 2 * Z)))
+
+
+def own_kernel(t_ref, p_ref, joined, kernel, o_ref, mine, work):
     z4, x8, y_in, y_out = views(joined)
-    odd = lax.axis_index("orb") % 2 == 1
+    z = z4[: 2 * Z, : 2 * Z]
     high = XB * HALF
     for step in range(GROUPS):
         rows, rows2 = chunk(step, high), chunk(step, high, X * HALF)
-        partner = jnp.concatenate(
-            [
-                spread_rows(p_ref[rows, :], p_ref[rows2, :]),
-                spread_rows(q_ref[rows, :], q_ref[rows2, :]),
-            ],
-            axis=1,
-        )
-        pairs[chunk(step, ROWS), :] = partner
-        work[pl.ds(step * XB, XB)] = inward(density(t_ref[rows, :], partner), z4, y_in)
-    middle(work, x8, kernel, 4 * Z)
-    for step in range(GROUPS):
-        partner = pairs[chunk(step, ROWS), :]
-        o_ref[pl.ds(step * XB, XB)] = outward(work, step, partner, odd, z4, y_out)
-
-
-def cross_kernel(r_ref, t_ref, c_ref, pairs, own_ref, joined, kernel, o_ref, work, first):
+        partner = spread_rows(p_ref[rows, :], p_ref[rows2, :])
+        mine[chunk(step, ROWS), :] = partner
+        work[pl.ds(step * XB, XB)] = inward(t_ref[rows, :], partner, z, y_in)
+    middle(work, x8, kernel, 2 * Z)
+    for step in range(GROUPS):
+        planes = pl.ds(step * XB, XB)
+        o_ref[planes] = outward(work[planes], mine[chunk(step, ROWS), :], z, y_out)
+
+
+def cross_kernel(r_ref, t_ref, c_ref, q_ref, mine, own_ref, joined, kernel, o_ref, work, pairs):
     z4, x8, y_in, y_out = views(joined)
     block = lax.axis_index("orb")
     half = lax.axis_size("orb") // 2
@@ -157,18 +149,16 @@
     for step in range(GROUPS):
         rows, rows2 = chunk(step, high), chunk(step, high, X * HALF)
         trial = jnp.where(even, r_ref[rows, :].astype(f32), t_ref[rows, :].astype(f32))
-        kept = pairs[chunk(step, ROWS), :]
-        carried = spread_rows(c_ref[rows, :], c_ref[rows2, :])
-        partner = jnp.where(even, kept[:, : 2 * Z].astype(f32), carried.astype(f32)).astype(bf16)
-        first[chunk(step, ROWS), :] = partner
-        partner = jnp.concatenate([partner, kept[:, 2 * Z :]], axis=1)
-        work[pl.ds(step * XB, XB)] = inward(density(trial, partner), z4, y_in)
+        carried = spread_rows(c_ref[rows, :], c_ref[rows2, :]).astype(f32)
+        first = jnp.where(even, mine[chunk(step, ROWS), :].astype(f32), carried).astype(bf16)
+        second = spread_rows(q_ref[rows, :], q_ref[rows2, :])
+        partner = jnp.concatenate([first, second], axis=1)
+        pairs[chunk(step, ROWS), :] = partner
+        work[pl.ds(step * XB, XB)] = inward(trial, partner, z4[...], y_in)
     middle(work, x8, kernel, 4 * Z)
     for step in range(GROUPS):
-        rows = chunk(step, ROWS)
-        partner = jnp.concatenate([first[rows, :], pairs[rows, 2 * Z :]], axis=1)
-        cross = outward(work, step, partner, even, z4, y_out)
         planes = pl.ds(step * XB, XB)
+        cross = outward(work[planes], pairs[chunk(step, ROWS), :], z4[...], y_out)
         own = own_ref[planes] + jnp.where(even, 0.0, cross)
         turned = jnp.concatenate([cross[i : i + 1] for i in reversed(range(XB))], axis=0)
         cross = jnp.where(border, turned, cross)
@@ -196,36 +186,35 @@
 
 
 COST = pl.CostEstimate(flops=4 * 10**9, bytes_accessed=3 * 10**6, transcendentals=0)
-WORK = pltpu.VMEM((X, Y, 4 * Z), f32)
-
-
-def own_call(trial, partner, other, tabs):
+
+
+def own_call(trial, partner, tabs):
     return pl.pallas_call(
         own_kernel,
         out_shape=(
             jax.ShapeDtypeStruct((X, HALF, 2 * Z), f32),
-            jax.ShapeDtypeStruct((X * Y, 4 * Z), bf16),
+            jax.ShapeDtypeStruct((X * Y, 2 * Z), bf16),
         ),
-        in_specs=[VMEM] * 5,
+        in_specs=[VMEM] * 4,
         out_specs=(VMEM, VMEM),
-        scratch_shapes=[WORK],
+        scratch_shapes=[pltpu.VMEM((X, Y, 2 * Z), f32)],
         cost_estimate=COST,
         compiler_params=GRANT,
         name="own_terms",
-    )(trial, partner, other, *tabs)
-
-
-def cross_call(remote, trial, carried, pairs, own, tabs):
+    )(trial, partner, *tabs)
+
+
+def cross_call(remote, trial, carried, other, mine, own, tabs):
     return pl.pallas_call(
         cross_kernel,
         out_shape=jax.ShapeDtypeStruct((X, Y, 2 * Z), bf16),
-        in_specs=[VMEM] * 7,
+        in_specs=[VMEM] * 8,
         out_specs=VMEM,
-        scratch_shapes=[WORK, pltpu.VMEM((X * Y, 2 * Z), bf16)],
+        scratch_shapes=[pltpu.VMEM((X, Y, 4 * Z), f32), pltpu.VMEM((X * Y, 4 * Z), bf16)],
         cost_estimate=COST,
         compiler_params=GRANT,
         name="cross_terms",
-    )(remote, trial, carried, pairs, own, *tabs)
+    )(remote, trial, carried, other, mine, own, *tabs)
 
 
 LOW = 4
@@ -254,8 +243,8 @@
     partner = as_rows(partners)
     carried = send(partner, 2, 1)
     other = lax.ppermute(partner, "orb", [(i ^ 1, i) for i in range(blocks)])
-    own, pairs = own_call(target, partner, other, tabs)
-    fields = cross_call(remote, target, carried, pairs, own, tabs)
+    own, mine = own_call(target, partner, tabs)
+    fields = cross_call(remote, target, carried, other, mine, own, tabs)
     slabs = lax.all_to_all(fields, "grp", 0, 0, tiled=True)
     summed = jnp.sum(slabs.astype(f32), axis=0)
     ahead = send(summed[HALF:], 2, 0)

time: 63.3 us -> 65.3 us (1.032)
  blocking collectives: 19.6 us -> 22.8 us
  waiting for transfers between devices: 10.1 us -> 6.99 us
  starting transfers between devices: 25.7 us -> 26.7 us
  Pallas kernels: 4.77 us -> 5.55 us
    all_to_all x1, blocking collectives: 19.6 us -> 22.8 us  [local(): slabs = lax.all_to_all(fields, 'grp', 0, 0, tiled=True)]
    ppermute x3, waiting for transfers between devices: 10.1 us -> 6.99 us  [local(): lax.ppermute(what, ('orb', 'grp'), route(blocks, groups, distance, parity))]
    ppermute x1, starting transfers between devices: 2.05 us -> 4.38 us  [local(): other = lax.ppermute(partner, 'orb', [(i ^ 1, i) for i in range(blocks)])]
    ppermute x3, starting transfers between devices: 23.6 us -> 22.4 us  [local(): lax.ppermute(what, ('orb', 'grp'), route(blocks, groups, distance, parity))]
    pallas_call x1, Pallas kernels: 2.35 us -> 3.1 us  [own_call(): pl.pallas_call(own_kernel, out_shape=(jax.ShapeDtypeStruct((X, HALF, 2 *...]
    unnamed x8 -> x10, local copies, waits for them, and re-layouts: 2.04 us -> 2.04 us
  transfers between devices with their start and end apart: 4 -> 4, of which waited for: 1 -> 1; matrix products, arithmetic and copies ran while one was open for 0% -> 0% of each run, Pallas kernels for 4% -> 5%
where the time goes in v7:
time: 65.3 us; the launch traced here: 65 us
  starting transfers between devices  26.7 us (41%)
  blocking collectives  22.8 us (35%)
  waiting for transfers between devices  6.99 us (11%)
  Pallas kernels  5.55 us (8%)
  local copies, waits for them, and re-layouts  2.05 us (3%)
  other arithmetic  0.67 us (1%)
    all_to_all x1, blocking collectives, local(): slabs = lax.all_to_all(fields, 'grp', 0, 0, tiled=True)  22.8 us
    ppermute x3, starting transfers between devices, local(): lax.ppermute(what, ('orb', 'grp'), route(blocks, groups, distance, parity))  22.4 us
    ppermute x3, waiting for transfers between devices, local(): lax.ppermute(what, ('orb', 'grp'), route(blocks, groups, distance, parity))  6.99 us
    ppermute x1, starting transfers between devices, local(): other = lax.ppermute(partner, 'orb', [(i ^ 1, i) for i in range(blocks)])  4.38 us
    pallas_call x1, Pallas kernels, own_call(): pl.pallas_call(own_kernel, out_shape=(jax.ShapeDtypeStruct((X, HALF, 2 *...  3.1 us
    pallas_call x1, Pallas kernels, cross_call(): pl.pallas_call(cross_kernel, out_shape=jax.ShapeDtypeStruct((X, Y, 2 * Z)...  2.37 us
    unnamed x10, local copies, waits for them, and re-layouts  2.04 us
  transfers between devices with their start and end apart: 4, of which 1 were waited for; matrix products, arithmetic and copies ran while one was open for 0% of the time, Pallas kernels for 5%

profile of v7, /device:TPU:2, one launch (start us, length us, event | category | flops | bytes accessed | tf_op | source)
XLA Modules:
  0.0 65.0 jit_solution(18049611622350759731)
XLA Ops:
  0.0 0.0 copy-start
  0.0 1.0 %copy-done = bf16[2,98304]{1,0:T(2,128)(2,1)S(1)} copy-done((bf16[2,98304]{1,0:T(2,128)(2,1)S(1)}, bf16[2,98304]{1,0:T(2,128)(2,1)}, u32[]{:S(2)}) %copy-start) | copy-done | bytes 393240
  1.0 0.0 copy-start.1
  1.0 0.0 copy-start.2
  1.0 0.1 as_rows.3.p_ref
  1.1 0.8 %collective-permute-start.1 = (bf16[1536,128]{1,0:T(8,128)(2,1)S(1)}, bf16[1536,128]{1,0:T(8,128)(2,1)S(1)}, u32[]{:S(2)}, u32[]{:S(2)}) collective-permute-start(bf16[1536,128]{1,0:T(8,128)(2,1)S(1)} %as_rows.3.p_ref), channel_id=1, source_target_pairs={{32,96},{33,97},{34,98},{35,99},{36,100},{37,101},{38,102},{39,103... | collective-permute-start | bytes 1179656 | tf_op jit(solution)/shard_map/ppermute | solution.py:237
  1.9 4.4 %collective-permute-start.2 = (bf16[1536,128]{1,0:T(8,128)(2,1)S(1)}, bf16[1536,128]{1,0:T(8,128)(2,1)S(1)}, u32[]{:S(2)}, u32[]{:S(2)}) collective-permute-start(bf16[1536,128]{1,0:T(8,128)(2,1)S(1)} %as_rows.3.p_ref), channel_id=1, source_target_pairs={{32,0},{0,32},{96,64},{64,96},{160,128},{128,160},{224,192},{192,2... | collective-permute-start | bytes 1179656 | tf_op jit(solution)/shard_map/ppermute | solution.py:245
  6.3 0.0 copy-done.1
  6.3 19.6 %collective-permute-start = (bf16[768,128]{1,0:T(8,128)(2,1)S(1)}, bf16[768,128]{1,0:T(8,128)(2,1)S(1)}, u32[]{:S(2)}, u32[]{:S(2)}) collective-permute-start(bf16[768,128]{1,0:T(8,128)(2,1)S(1)} %as_rows.2.t_ref), channel_id=1, source_target_pairs={{0,963},{1,962},{2,961},{3,960},{4,967},{5,966},{6,965},{7,964},{8... | collective-permute-start | bytes 589832 | tf_op jit(solution)/shard_map/ppermute | solution.py:237
  25.9 0.0 copy-done.2
  26.0 0.0 copy-start.3
  26.0 1.0 %copy-done.3 = bf16[256,1024]{1,0:T(8,128)(2,1)S(1)} copy-done((bf16[256,1024]{1,0:T(8,128)(2,1)S(1)}, bf16[256,1024]{1,0:T(8,128)(2,1)}, u32[]{:S(2)}) %copy-start.3) | copy-done | bytes 524312
  27.0 0.0 copy-start.4
  27.0 3.1 %own_terms.1 = (f32[32,24,128]{2,1,0:T(8,128)S(1)}, bf16[1536,128]{1,0:T(8,128)(2,1)S(1)}) custom-call(bf16[768,128]{1,0:T(8,128)(2,1)S(1)} %as_rows.2.t_ref, bf16[1536,128]{1,0:T(8,128)(2,1)S(1)} %as_rows.3.p_ref, bf16[256,1024]{1,0:T(8,128)(2,1)S(1)} %copy-done.3, f32[32,48,128]{2,1,0:T(8,128)S(1)} %copy-done.2), custom_call_target="tpu_custom_call" | custom-call | flops 4000000000 | bytes 3000000 | tf_op jit(solution)/shard_map/own_terms/pallas_call | solution.py:192
  30.1 0.0 collective-permute-done.r_ref
  30.1 0.0 collective-permute-done.1.c_ref
  30.1 0.0 collective-permute-done.2.q_ref
  30.1 0.0 copy-done.4
  30.1 2.4 %cross_terms.1 = bf16[32,48,128]{2,1,0:T(8,128)(2,1)S(1)} custom-call(bf16[768,128]{1,0:T(8,128)(2,1)S(1)} %collective-permute-done.r_ref, bf16[768,128]{1,0:T(8,128)(2,1)S(1)} %as_rows.2.t_ref, bf16[1536,128]{1,0:T(8,128)(2,1)S(1)} %collective-permute-done.1.c_ref, bf16[1536,128]{1,0:T(8,128)(2,1)S(1)} %collective-permute-done.2.q_ref, ...), custom_call_target="tpu_custom_call" | custom-call | flops 4000000000 | bytes 3000000 | tf_op jit(solution)/shard_map/cross_terms/pallas_call | solution.py:208
  32.5 22.8 %all_to_all.5 = bf16[32,48,128]{2,1,0:T(8,128)(2,1)S(1)} all-to-all(bf16[32,48,128]{2,1,0:T(8,128)(2,1)S(1)} %cross_terms.1), channel_id=1, replica_groups=mesh['orb'=32,'grp'=32] {'grp'}, dimensions={0} | all-to-all | bytes 786432 | tf_op jit(solution)/shard_map/all_to_all | solution.py:248
  55.4 0.1 convert_reduce_fusion
  55.4 1.9 %collective-permute-start.3 = (f32[24,128]{1,0:T(8,128)S(1)}, f32[24,128]{1,0:T(8,128)S(1)}, u32[]{:S(2)}, u32[]{:S(2)}) collective-permute-start(f32[24,128]{1,0:T(8,128)S(1)} %slice.9), channel_id=1, source_target_pairs={{0,64},{1,65},{2,66},{3,67},{4,68},{5,69},{6,70},{7,71},{8,72},{9,... | collective-permute-start | bytes 36872 | tf_op jit(solution)/shard_map/ppermute | solution.py:237
  57.4 7.0 %collective-permute-done.3 = f32[24,128]{1,0:T(8,128)S(1)} collective-permute-done((f32[24,128]{1,0:T(8,128)S(1)}, f32[24,128]{1,0:T(8,128)S(1)}, u32[]{:S(2)}, u32[]{:S(2)}) %collective-permute-start.3) | collective-permute-done | bytes 12320 | tf_op jit(solution)/shard_map/ppermute | solution.py:237
  64.3 0.6 fusion
  (2 shorter events, 0.0 us)
Async XLA Ops:
  0.0 1.0 %copy-start = (bf16[2,98304]{1,0:T(2,128)(2,1)S(1)}, bf16[2,98304]{1,0:T(2,128)(2,1)}, u32[]{:S(2)}) copy-start(bf16[2,98304]{1,0:T(2,128)(2,1)} %x_ref.3) | copy-start | bytes 1179652
  1.0 5.3 %copy-start.1 = (bf16[1,98304]{1,0:T(2,128)(2,1)S(1)}, bf16[1,98304]{1,0:T(2,128)(2,1)}, u32[]{:S(2)}) copy-start(bf16[1,98304]{1,0:T(2,128)(2,1)} %x_ref.2) | copy-start | bytes 589828
  1.0 24.9 %copy-start.2 = (f32[32,48,128]{2,1,0:T(8,128)S(1)}, f32[32,48,128]{2,1,0:T(8,128)}, u32[]{:S(2)}) copy-start(f32[32,48,128]{2,1,0:T(8,128)} %constant.8.clone.kernel) | copy-start | bytes 2359300
  1.1 29.1 %collective-permute-start.1 = (bf16[1536,128]{1,0:T(8,128)(2,1)S(1)}, bf16[1536,128]{1,0:T(8,128)(2,1)S(1)}, u32[]{:S(2)}, u32[]{:S(2)}) collective-permute-start(bf16[1536,128]{1,0:T(8,128)(2,1)S(1)} %as_rows.3.p_ref), channel_id=1, source_target_pairs={{32,96},{33,97},{34,98},{35,99},{36,100},{37,101},{38,102},{39,103... | collective-permute-start | bytes 1179656 | tf_op jit(solution)/shard_map/ppermute | solution.py:237
  1.9 28.2 %collective-permute-start.2 = (bf16[1536,128]{1,0:T(8,128)(2,1)S(1)}, bf16[1536,128]{1,0:T(8,128)(2,1)S(1)}, u32[]{:S(2)}, u32[]{:S(2)}) collective-permute-start(bf16[1536,128]{1,0:T(8,128)(2,1)S(1)} %as_rows.3.p_ref), channel_id=1, source_target_pairs={{32,0},{0,32},{96,64},{64,96},{160,128},{128,160},{224,192},{192,2... | collective-permute-start | bytes 1179656 | tf_op jit(solution)/shard_map/ppermute | solution.py:245
  6.3 23.8 %collective-permute-start = (bf16[768,128]{1,0:T(8,128)(2,1)S(1)}, bf16[768,128]{1,0:T(8,128)(2,1)S(1)}, u32[]{:S(2)}, u32[]{:S(2)}) collective-permute-start(bf16[768,128]{1,0:T(8,128)(2,1)S(1)} %as_rows.2.t_ref), channel_id=1, source_target_pairs={{0,963},{1,962},{2,961},{3,960},{4,967},{5,966},{6,965},{7,964},{8... | collective-permute-start | bytes 589832 | tf_op jit(solution)/shard_map/ppermute | solution.py:237
  26.0 1.0 %copy-start.3 = (bf16[256,1024]{1,0:T(8,128)(2,1)S(1)}, bf16[256,1024]{1,0:T(8,128)(2,1)}, u32[]{:S(2)}) copy-start(bf16[256,1024]{1,0:T(8,128)(2,1)} %constant.9.clone.joined) | copy-start | bytes 1572868
  27.0 3.1 %copy-start.4 = (bf16[256,1024]{1,0:T(8,128)(2,1)S(1)}, bf16[256,1024]{1,0:T(8,128)(2,1)}, u32[]{:S(2)}) copy-start(bf16[256,1024]{1,0:T(8,128)(2,1)} %constant.9.clone.joined) | copy-start | bytes 1572868
  55.4 8.9 %collective-permute-start.3 = (f32[24,128]{1,0:T(8,128)S(1)}, f32[24,128]{1,0:T(8,128)S(1)}, u32[]{:S(2)}, u32[]{:S(2)}) collective-permute-start(f32[24,128]{1,0:T(8,128)S(1)} %slice.9), channel_id=1, source_target_pairs={{0,64},{1,65},{2,66},{3,67},{4,68},{5,69},{6,70},{7,71},{8,72},{9,... | collective-permute-start | bytes 36872 | tf_op jit(solution)/shard_map/ppermute | solution.py:237

commit v8 on v7

--- a/solution.py
+++ b/solution.py
@@ -97,14 +97,16 @@
 
 
 def middle(work, x8, kernel, lanes):
-    for block in range(Y // 8):
-        rows = slice(block * 8, block * 8 + 8)
-        field = work[:, rows, :].reshape(X * 8, lanes).astype(bf16)
-        scale = kernel[:, rows, :].reshape(X * 8, 2 * Z)
-        scale = jnp.concatenate([scale] * (lanes // (2 * Z)), axis=1)
-        field = dot(x8[...], field)
+    together = 4 * Z // lanes
+    for block in range(0, Y // 8, together):
+        groups = [slice(at * 8, at * 8 + 8) for at in range(block, block + together)]
+        field = jnp.concatenate([work[:, g, :].reshape(X * 8, lanes) for g in groups], axis=1)
+        scale = [kernel[:, g, :].reshape(X * 8, 2 * Z) for g in groups]
+        scale = jnp.concatenate([t for t in scale for _ in range(lanes // (2 * Z))], axis=1)
+        field = dot(x8[...], field.astype(bf16))
         field = dot(x8[...], (field * scale).astype(bf16))
-        work[:, rows, :] = field.reshape(X, 8, lanes)
+        for at, g in enumerate(groups):
+            work[:, g, :] = field[:, at * lanes : (at + 1) * lanes].reshape(X, 8, lanes)
 
 
 def chunk(step, high, base=0):
@@ -126,17 +128,27 @@
 
 def own_kernel(t_ref, p_ref, joined, kernel, o_ref, mine, work):
     z4, x8, y_in, y_out = views(joined)
-    z = z4[: 2 * Z, : 2 * Z]
     high = XB * HALF
-    for step in range(GROUPS):
-        rows, rows2 = chunk(step, high), chunk(step, high, X * HALF)
-        partner = spread_rows(p_ref[rows, :], p_ref[rows2, :])
-        mine[chunk(step, ROWS), :] = partner
-        work[pl.ds(step * XB, XB)] = inward(t_ref[rows, :], partner, z, y_in)
+    halves = [slice(0, 2 * Z), slice(2 * Z, 4 * Z)]
+    for step in range(0, GROUPS, 2):
+        density = []
+        for at in (step, step + 1):
+            rows, rows2 = chunk(at, high), chunk(at, high, X * HALF)
+            partner = spread_rows(p_ref[rows, :], p_ref[rows2, :])
+            mine[chunk(at, ROWS), :] = partner
+            density.append(spread_rows(t_ref[rows, :], t_ref[rows, :]) * partner)
+        field = dot(jnp.concatenate(density, axis=1), z4[...]).astype(bf16)
+        field = dot(y_in[...], field)
+        for at, lanes in zip((step, step + 1), halves):
+            work[pl.ds(at * XB, XB)] = field[:, lanes].reshape(XB, Y, 2 * Z)
     middle(work, x8, kernel, 2 * Z)
-    for step in range(GROUPS):
-        planes = pl.ds(step * XB, XB)
-        o_ref[planes] = outward(work[planes], mine[chunk(step, ROWS), :], z, y_out)
+    for step in range(0, GROUPS, 2):
+        field = [work[pl.ds(at * XB, XB)].reshape(ROWS, 2 * Z) for at in (step, step + 1)]
+        field = jnp.concatenate(field, axis=1).astype(bf16)
+        field = dot(dot(y_out[...], field).astype(bf16), z4[...])
+        for at, lanes in zip((step, step + 1), halves):
+            partner = mine[chunk(at, ROWS), :].astype(f32)
+            o_ref[pl.ds(at * XB, XB)] = gather_rows(field[:, lanes] * partner)
 
 
 def cross_kernel(r_ref, t_ref, c_ref, q_ref, mine, own_ref, joined, kernel, o_ref, work, pairs):

time: 65.3 us -> 64.7 us (level)
  the two profiles are of different devices: /device:TPU:2 before, /device:TPU:4 now
where the time goes in v8:
time: 64.7 us; the launch traced here: 64.4 us
  starting transfers between devices  26.7 us (41%)
  blocking collectives  23.3 us (36%)
  waiting for transfers between devices  7.38 us (11%)
  Pallas kernels  4.16 us (6%)
  local copies, waits for them, and re-layouts  2.05 us (3%)
  other arithmetic  0.67 us (1%)
    all_to_all x1, blocking collectives, local(): slabs = lax.all_to_all(fields, 'grp', 0, 0, tiled=True)  23.3 us
    ppermute x3, starting transfers between devices, local(): lax.ppermute(what, ('orb', 'grp'), route(blocks, groups, distance, parity))  22.4 us
    ppermute x3, waiting for transfers between devices, local(): lax.ppermute(what, ('orb', 'grp'), route(blocks, groups, distance, parity))  7.38 us
    ppermute x1, starting transfers between devices, local(): other = lax.ppermute(partner, 'orb', [(i ^ 1, i) for i in range(blocks)])  4.38 us
    pallas_call x1, Pallas kernels, cross_call(): pl.pallas_call(cross_kernel, out_shape=jax.ShapeDtypeStruct((X, Y, 2 * Z)...  2.37 us
    unnamed x10, local copies, waits for them, and re-layouts  2.04 us
    pallas_call x1, Pallas kernels, own_call(): pl.pallas_call(own_kernel, out_shape=(jax.ShapeDtypeStruct((X, HALF, 2 *...  1.71 us
  transfers between devices with their start and end apart: 4, of which 2 were waited for; matrix products, arithmetic and copies ran while one was open for 0% of the time, Pallas kernels for 3%

profile of v8, /device:TPU:4, one launch (start us, length us, event | category | flops | bytes accessed | tf_op | source)
XLA Modules:
  0.0 64.4 jit_solution(6686567483622913538)
XLA Ops:
  0.0 0.0 copy-start
  0.0 1.0 %copy-done = bf16[2,98304]{1,0:T(2,128)(2,1)S(1)} copy-done((bf16[2,98304]{1,0:T(2,128)(2,1)S(1)}, bf16[2,98304]{1,0:T(2,128)(2,1)}, u32[]{:S(2)}) %copy-start) | copy-done | bytes 393240
  1.0 0.0 copy-start.1
  1.0 0.0 copy-start.2
  1.0 0.1 as_rows.3.p_ref
  1.1 0.8 %collective-permute-start.1 = (bf16[1536,128]{1,0:T(8,128)(2,1)S(1)}, bf16[1536,128]{1,0:T(8,128)(2,1)S(1)}, u32[]{:S(2)}, u32[]{:S(2)}) collective-permute-start(bf16[1536,128]{1,0:T(8,128)(2,1)S(1)} %as_rows.3.p_ref), channel_id=1, source_target_pairs={{32,96},{33,97},{34,98},{35,99},{36,100},{37,101},{38,102},{39,103... | collective-permute-start | bytes 1179656 | tf_op jit(solution)/shard_map/ppermute | solution.py:249
  1.9 4.4 %collective-permute-start.2 = (bf16[1536,128]{1,0:T(8,128)(2,1)S(1)}, bf16[1536,128]{1,0:T(8,128)(2,1)S(1)}, u32[]{:S(2)}, u32[]{:S(2)}) collective-permute-start(bf16[1536,128]{1,0:T(8,128)(2,1)S(1)} %as_rows.3.p_ref), channel_id=1, source_target_pairs={{32,0},{0,32},{96,64},{64,96},{160,128},{128,160},{224,192},{192,2... | collective-permute-start | bytes 1179656 | tf_op jit(solution)/shard_map/ppermute | solution.py:257
  6.3 0.0 copy-done.1
  6.3 19.6 %collective-permute-start = (bf16[768,128]{1,0:T(8,128)(2,1)S(1)}, bf16[768,128]{1,0:T(8,128)(2,1)S(1)}, u32[]{:S(2)}, u32[]{:S(2)}) collective-permute-start(bf16[768,128]{1,0:T(8,128)(2,1)S(1)} %as_rows.2.t_ref), channel_id=1, source_target_pairs={{0,963},{1,962},{2,961},{3,960},{4,967},{5,966},{6,965},{7,964},{8... | collective-permute-start | bytes 589832 | tf_op jit(solution)/shard_map/ppermute | solution.py:249
  25.9 0.0 copy-done.2
  26.0 0.0 copy-start.3
  26.0 1.0 %copy-done.3 = bf16[256,1024]{1,0:T(8,128)(2,1)S(1)} copy-done((bf16[256,1024]{1,0:T(8,128)(2,1)S(1)}, bf16[256,1024]{1,0:T(8,128)(2,1)}, u32[]{:S(2)}) %copy-start.3) | copy-done | bytes 524312
  27.0 0.0 copy-start.4
  27.0 1.7 %own_terms.1 = (f32[32,24,128]{2,1,0:T(8,128)S(1)}, bf16[1536,128]{1,0:T(8,128)(2,1)S(1)}) custom-call(bf16[768,128]{1,0:T(8,128)(2,1)S(1)} %as_rows.2.t_ref, bf16[1536,128]{1,0:T(8,128)(2,1)S(1)} %as_rows.3.p_ref, bf16[256,1024]{1,0:T(8,128)(2,1)S(1)} %copy-done.3, f32[32,48,128]{2,1,0:T(8,128)S(1)} %copy-done.2), custom_call_target="tpu_custom_call" | custom-call | flops 4000000000 | bytes 3000000 | tf_op jit(solution)/shard_map/own_terms/pallas_call | solution.py:204
  28.7 0.4 collective-permute-done.r_ref
  29.1 0.0 collective-permute-done.1.c_ref
  29.1 0.0 collective-permute-done.2.q_ref
  29.1 0.0 copy-done.4
  29.1 2.4 %cross_terms.1 = bf16[32,48,128]{2,1,0:T(8,128)(2,1)S(1)} custom-call(bf16[768,128]{1,0:T(8,128)(2,1)S(1)} %collective-permute-done.r_ref, bf16[768,128]{1,0:T(8,128)(2,1)S(1)} %as_rows.2.t_ref, bf16[1536,128]{1,0:T(8,128)(2,1)S(1)} %collective-permute-done.1.c_ref, bf16[1536,128]{1,0:T(8,128)(2,1)S(1)} %collective-permute-done.2.q_ref, ...), custom_call_target="tpu_custom_call" | custom-call | flops 4000000000 | bytes 3000000 | tf_op jit(solution)/shard_map/cross_terms/pallas_call | solution.py:220
  31.5 23.3 %all_to_all.5 = bf16[32,48,128]{2,1,0:T(8,128)(2,1)S(1)} all-to-all(bf16[32,48,128]{2,1,0:T(8,128)(2,1)S(1)} %cross_terms.1), channel_id=1, replica_groups=mesh['orb'=32,'grp'=32] {'grp'}, dimensions={0} | all-to-all | bytes 786432 | tf_op jit(solution)/shard_map/all_to_all | solution.py:260
  54.8 0.1 convert_reduce_fusion
  54.9 1.9 %collective-permute-start.3 = (f32[24,128]{1,0:T(8,128)S(1)}, f32[24,128]{1,0:T(8,128)S(1)}, u32[]{:S(2)}, u32[]{:S(2)}) collective-permute-start(f32[24,128]{1,0:T(8,128)S(1)} %slice.9), channel_id=1, source_target_pairs={{0,64},{1,65},{2,66},{3,67},{4,68},{5,69},{6,70},{7,71},{8,72},{9,... | collective-permute-start | bytes 36872 | tf_op jit(solution)/shard_map/ppermute | solution.py:249
  56.8 7.0 %collective-permute-done.3 = f32[24,128]{1,0:T(8,128)S(1)} collective-permute-done((f32[24,128]{1,0:T(8,128)S(1)}, f32[24,128]{1,0:T(8,128)S(1)}, u32[]{:S(2)}, u32[]{:S(2)}) %collective-permute-start.3) | collective-permute-done | bytes 12320 | tf_op jit(solution)/shard_map/ppermute | solution.py:249
  63.8 0.6 fusion
  (2 shorter events, 0.0 us)
Async XLA Ops:
  0.0 1.0 %copy-start = (bf16[2,98304]{1,0:T(2,128)(2,1)S(1)}, bf16[2,98304]{1,0:T(2,128)(2,1)}, u32[]{:S(2)}) copy-start(bf16[2,98304]{1,0:T(2,128)(2,1)} %x_ref.3) | copy-start | bytes 1179652
  1.0 5.3 %copy-start.1 = (bf16[1,98304]{1,0:T(2,128)(2,1)S(1)}, bf16[1,98304]{1,0:T(2,128)(2,1)}, u32[]{:S(2)}) copy-start(bf16[1,98304]{1,0:T(2,128)(2,1)} %x_ref.2) | copy-start | bytes 589828
  1.0 24.9 %copy-start.2 = (f32[32,48,128]{2,1,0:T(8,128)S(1)}, f32[32,48,128]{2,1,0:T(8,128)}, u32[]{:S(2)}) copy-start(f32[32,48,128]{2,1,0:T(8,128)} %constant.8.clone.kernel) | copy-start | bytes 2359300
  1.1 28.1 %collective-permute-start.1 = (bf16[1536,128]{1,0:T(8,128)(2,1)S(1)}, bf16[1536,128]{1,0:T(8,128)(2,1)S(1)}, u32[]{:S(2)}, u32[]{:S(2)}) collective-permute-start(bf16[1536,128]{1,0:T(8,128)(2,1)S(1)} %as_rows.3.p_ref), channel_id=1, source_target_pairs={{32,96},{33,97},{34,98},{35,99},{36,100},{37,101},{38,102},{39,103... | collective-permute-start | bytes 1179656 | tf_op jit(solution)/shard_map/ppermute | solution.py:249
  1.9 27.2 %collective-permute-start.2 = (bf16[1536,128]{1,0:T(8,128)(2,1)S(1)}, bf16[1536,128]{1,0:T(8,128)(2,1)S(1)}, u32[]{:S(2)}, u32[]{:S(2)}) collective-permute-start(bf16[1536,128]{1,0:T(8,128)(2,1)S(1)} %as_rows.3.p_ref), channel_id=1, source_target_pairs={{32,0},{0,32},{96,64},{64,96},{160,128},{128,160},{224,192},{192,2... | collective-permute-start | bytes 1179656 | tf_op jit(solution)/shard_map/ppermute | solution.py:257
  6.3 22.8 %collective-permute-start = (bf16[768,128]{1,0:T(8,128)(2,1)S(1)}, bf16[768,128]{1,0:T(8,128)(2,1)S(1)}, u32[]{:S(2)}, u32[]{:S(2)}) collective-permute-start(bf16[768,128]{1,0:T(8,128)(2,1)S(1)} %as_rows.2.t_ref), channel_id=1, source_target_pairs={{0,963},{1,962},{2,961},{3,960},{4,967},{5,966},{6,965},{7,964},{8... | collective-permute-start | bytes 589832 | tf_op jit(solution)/shard_map/ppermute | solution.py:249
  26.0 1.0 %copy-start.3 = (bf16[256,1024]{1,0:T(8,128)(2,1)S(1)}, bf16[256,1024]{1,0:T(8,128)(2,1)}, u32[]{:S(2)}) copy-start(bf16[256,1024]{1,0:T(8,128)(2,1)} %constant.9.clone.joined) | copy-start | bytes 1572868
  27.0 2.1 %copy-start.4 = (bf16[256,1024]{1,0:T(8,128)(2,1)S(1)}, bf16[256,1024]{1,0:T(8,128)(2,1)}, u32[]{:S(2)}) copy-start(bf16[256,1024]{1,0:T(8,128)(2,1)} %constant.9.clone.joined) | copy-start | bytes 1572868
  54.9 8.9 %collective-permute-start.3 = (f32[24,128]{1,0:T(8,128)S(1)}, f32[24,128]{1,0:T(8,128)S(1)}, u32[]{:S(2)}, u32[]{:S(2)}) collective-permute-start(f32[24,128]{1,0:T(8,128)S(1)} %slice.9), channel_id=1, source_target_pairs={{0,64},{1,65},{2,66},{3,67},{4,68},{5,69},{6,70},{7,71},{8,72},{9,... | collective-permute-start | bytes 36872 | tf_op jit(solution)/shard_map/ppermute | solution.py:249

commit v9 on v8

--- a/solution.py
+++ b/solution.py
@@ -232,26 +232,28 @@
 LOW = 4
 
 
-def route(blocks, groups, distance, parity):
+def route(blocks, groups, distance, parity, cycle=False):
     half = blocks // 2
     pairs = []
     for block in range(parity, blocks, 2):
         target = (block + distance) % blocks
         for group in range(groups):
-            mirror = group // LOW * LOW + LOW - 1 - group % LOW
-            place = mirror if target // half != block // half else group
+            place = group % LOW
+            if target // half != block // half:
+                place = LOW - 1 - place
+                if cycle:
+                    place = (group + (1 if block >= half else LOW - 1)) % LOW
+            place += group // LOW * LOW
             pairs.append((block * groups + group, target * groups + place))
     return pairs
 
 
 def local(targets, partners):
     blocks, groups = lax.axis_size("orb"), lax.axis_size("grp")
-    send = lambda what, distance, parity: lax.ppermute(
-        what, ("orb", "grp"), route(blocks, groups, distance, parity)
-    )
+    send = lambda what, *how: lax.ppermute(what, ("orb", "grp"), route(blocks, groups, *how))
     tabs = tables()
     target = as_rows(targets)
-    remote = send(target, -2, 0)
+    remote = send(target, -2, 0, True)
     partner = as_rows(partners)
     carried = send(partner, 2, 1)
     other = lax.ppermute(partner, "orb", [(i ^ 1, i) for i in range(blocks)])

time: 64.7 us -> 65.3 us (level)
  the two profiles are of different devices: /device:TPU:4 before, /device:TPU:2 now
where the time goes in v9:
time: 65.3 us; the launch traced here: 65 us
  starting transfers between devices  26.7 us (41%)
  blocking collectives  23.9 us (37%)
  waiting for transfers between devices  7.38 us (11%)
  Pallas kernels  4.16 us (6%)
  local copies, waits for them, and re-layouts  2.05 us (3%)
  other arithmetic  0.67 us (1%)
    all_to_all x1, blocking collectives, local(): slabs = lax.all_to_all(fields, 'grp', 0, 0, tiled=True)  23.9 us
    ppermute x3, starting transfers between devices, local(): lax.ppermute(what, ('orb', 'grp'), route(blocks, groups, *how))  22.4 us
    ppermute x3, waiting for transfers between devices, local(): lax.ppermute(what, ('orb', 'grp'), route(blocks, groups, *how))  7.38 us
    ppermute x1, starting transfers between devices, local(): other = lax.ppermute(partner, 'orb', [(i ^ 1, i) for i in range(blocks)])  4.38 us
    pallas_call x1, Pallas kernels, cross_call(): pl.pallas_call(cross_kernel, out_shape=jax.ShapeDtypeStruct((X, Y, 2 * Z)...  2.37 us
    unnamed x10, local copies, waits for them, and re-layouts  2.04 us
    pallas_call x1, Pallas kernels, own_call(): pl.pallas_call(own_kernel, out_shape=(jax.ShapeDtypeStruct((X, HALF, 2 *...  1.7 us
  transfers between devices with their start and end apart: 4, of which 2 were waited for; matrix products, arithmetic and copies ran while one was open for 0% of the time, Pallas kernels for 3%

profile of v9, /device:TPU:2, one launch (start us, length us, event | category | flops | bytes accessed | tf_op | source)
XLA Modules:
  0.0 65.0 jit_solution(18340449172325421539)
XLA Ops:
  0.0 0.0 copy-start
  0.0 1.0 %copy-done = bf16[2,98304]{1,0:T(2,128)(2,1)S(1)} copy-done((bf16[2,98304]{1,0:T(2,128)(2,1)S(1)}, bf16[2,98304]{1,0:T(2,128)(2,1)}, u32[]{:S(2)}) %copy-start) | copy-done | bytes 393240
  1.0 0.0 copy-start.1
  1.0 0.0 copy-start.2
  1.0 0.1 as_rows.3.p_ref
  1.1 0.8 %collective-permute-start.1 = (bf16[1536,128]{1,0:T(8,128)(2,1)S(1)}, bf16[1536,128]{1,0:T(8,128)(2,1)S(1)}, u32[]{:S(2)}, u32[]{:S(2)}) collective-permute-start(bf16[1536,128]{1,0:T(8,128)(2,1)S(1)} %as_rows.3.p_ref), channel_id=1, source_target_pairs={{32,96},{33,97},{34,98},{35,99},{36,100},{37,101},{38,102},{39,103... | collective-permute-start | bytes 1179656 | tf_op jit(solution)/shard_map/ppermute | solution.py:253
  1.9 4.4 %collective-permute-start.2 = (bf16[1536,128]{1,0:T(8,128)(2,1)S(1)}, bf16[1536,128]{1,0:T(8,128)(2,1)S(1)}, u32[]{:S(2)}, u32[]{:S(2)}) collective-permute-start(bf16[1536,128]{1,0:T(8,128)(2,1)S(1)} %as_rows.3.p_ref), channel_id=1, source_target_pairs={{32,0},{0,32},{96,64},{64,96},{160,128},{128,160},{224,192},{192,2... | collective-permute-start | bytes 1179656 | tf_op jit(solution)/shard_map/ppermute | solution.py:259
  6.3 0.0 copy-done.1
  6.3 19.6 %collective-permute-start = (bf16[768,128]{1,0:T(8,128)(2,1)S(1)}, bf16[768,128]{1,0:T(8,128)(2,1)S(1)}, u32[]{:S(2)}, u32[]{:S(2)}) collective-permute-start(bf16[768,128]{1,0:T(8,128)(2,1)S(1)} %as_rows.2.t_ref), channel_id=1, source_target_pairs={{0,963},{1,960},{2,961},{3,962},{4,967},{5,964},{6,965},{7,966},{8... | collective-permute-start | bytes 589832 | tf_op jit(solution)/shard_map/ppermute | solution.py:253
  25.9 0.0 copy-done.2
  26.0 0.0 copy-start.3
  26.0 1.0 %copy-done.3 = bf16[256,1024]{1,0:T(8,128)(2,1)S(1)} copy-done((bf16[256,1024]{1,0:T(8,128)(2,1)S(1)}, bf16[256,1024]{1,0:T(8,128)(2,1)}, u32[]{:S(2)}) %copy-start.3) | copy-done | bytes 524312
  27.0 0.0 copy-start.4
  27.0 1.7 %own_terms.1 = (f32[32,24,128]{2,1,0:T(8,128)S(1)}, bf16[1536,128]{1,0:T(8,128)(2,1)S(1)}) custom-call(bf16[768,128]{1,0:T(8,128)(2,1)S(1)} %as_rows.2.t_ref, bf16[1536,128]{1,0:T(8,128)(2,1)S(1)} %as_rows.3.p_ref, bf16[256,1024]{1,0:T(8,128)(2,1)S(1)} %copy-done.3, f32[32,48,128]{2,1,0:T(8,128)S(1)} %copy-done.2), custom_call_target="tpu_custom_call" | custom-call | flops 4000000000 | bytes 3000000 | tf_op jit(solution)/shard_map/own_terms/pallas_call | solution.py:204
  28.7 0.4 collective-permute-done.r_ref
  29.1 0.0 collective-permute-done.1.c_ref
  29.1 0.0 collective-permute-done.2.q_ref
  29.1 0.0 copy-done.4
  29.1 2.4 %cross_terms.1 = bf16[32,48,128]{2,1,0:T(8,128)(2,1)S(1)} custom-call(bf16[768,128]{1,0:T(8,128)(2,1)S(1)} %collective-permute-done.r_ref, bf16[768,128]{1,0:T(8,128)(2,1)S(1)} %as_rows.2.t_ref, bf16[1536,128]{1,0:T(8,128)(2,1)S(1)} %collective-permute-done.1.c_ref, bf16[1536,128]{1,0:T(8,128)(2,1)S(1)} %collective-permute-done.2.q_ref, ...), custom_call_target="tpu_custom_call" | custom-call | flops 4000000000 | bytes 3000000 | tf_op jit(solution)/shard_map/cross_terms/pallas_call | solution.py:220
  31.5 23.9 %all_to_all.5 = bf16[32,48,128]{2,1,0:T(8,128)(2,1)S(1)} all-to-all(bf16[32,48,128]{2,1,0:T(8,128)(2,1)S(1)} %cross_terms.1), channel_id=1, replica_groups=mesh['orb'=32,'grp'=32] {'grp'}, dimensions={0} | all-to-all | bytes 786432 | tf_op jit(solution)/shard_map/all_to_all | solution.py:262
  55.4 0.1 convert_reduce_fusion
  55.4 1.9 %collective-permute-start.3 = (f32[24,128]{1,0:T(8,128)S(1)}, f32[24,128]{1,0:T(8,128)S(1)}, u32[]{:S(2)}, u32[]{:S(2)}) collective-permute-start(f32[24,128]{1,0:T(8,128)S(1)} %slice.9), channel_id=1, source_target_pairs={{0,64},{1,65},{2,66},{3,67},{4,68},{5,69},{6,70},{7,71},{8,72},{9,... | collective-permute-start | bytes 36872 | tf_op jit(solution)/shard_map/ppermute | solution.py:253
  57.4 7.0 %collective-permute-done.3 = f32[24,128]{1,0:T(8,128)S(1)} collective-permute-done((f32[24,128]{1,0:T(8,128)S(1)}, f32[24,128]{1,0:T(8,128)S(1)}, u32[]{:S(2)}, u32[]{:S(2)}) %collective-permute-start.3) | collective-permute-done | bytes 12320 | tf_op jit(solution)/shard_map/ppermute | solution.py:253
  64.3 0.6 fusion
  (2 shorter events, 0.0 us)
Async XLA Ops:
  0.0 1.0 %copy-start = (bf16[2,98304]{1,0:T(2,128)(2,1)S(1)}, bf16[2,98304]{1,0:T(2,128)(2,1)}, u32[]{:S(2)}) copy-start(bf16[2,98304]{1,0:T(2,128)(2,1)} %x_ref.3) | copy-start | bytes 1179652
  1.0 5.3 %copy-start.1 = (bf16[1,98304]{1,0:T(2,128)(2,1)S(1)}, bf16[1,98304]{1,0:T(2,128)(2,1)}, u32[]{:S(2)}) copy-start(bf16[1,98304]{1,0:T(2,128)(2,1)} %x_ref.2) | copy-start | bytes 589828
  1.0 24.9 %copy-start.2 = (f32[32,48,128]{2,1,0:T(8,128)S(1)}, f32[32,48,128]{2,1,0:T(8,128)}, u32[]{:S(2)}) copy-start(f32[32,48,128]{2,1,0:T(8,128)} %constant.8.clone.kernel) | copy-start | bytes 2359300
  1.1 28.1 %collective-permute-start.1 = (bf16[1536,128]{1,0:T(8,128)(2,1)S(1)}, bf16[1536,128]{1,0:T(8,128)(2,1)S(1)}, u32[]{:S(2)}, u32[]{:S(2)}) collective-permute-start(bf16[1536,128]{1,0:T(8,128)(2,1)S(1)} %as_rows.3.p_ref), channel_id=1, source_target_pairs={{32,96},{33,97},{34,98},{35,99},{36,100},{37,101},{38,102},{39,103... | collective-permute-start | bytes 1179656 | tf_op jit(solution)/shard_map/ppermute | solution.py:253
  1.9 27.2 %collective-permute-start.2 = (bf16[1536,128]{1,0:T(8,128)(2,1)S(1)}, bf16[1536,128]{1,0:T(8,128)(2,1)S(1)}, u32[]{:S(2)}, u32[]{:S(2)}) collective-permute-start(bf16[1536,128]{1,0:T(8,128)(2,1)S(1)} %as_rows.3.p_ref), channel_id=1, source_target_pairs={{32,0},{0,32},{96,64},{64,96},{160,128},{128,160},{224,192},{192,2... | collective-permute-start | bytes 1179656 | tf_op jit(solution)/shard_map/ppermute | solution.py:259
  6.3 22.8 %collective-permute-start = (bf16[768,128]{1,0:T(8,128)(2,1)S(1)}, bf16[768,128]{1,0:T(8,128)(2,1)S(1)}, u32[]{:S(2)}, u32[]{:S(2)}) collective-permute-start(bf16[768,128]{1,0:T(8,128)(2,1)S(1)} %as_rows.2.t_ref), channel_id=1, source_target_pairs={{0,963},{1,960},{2,961},{3,962},{4,967},{5,964},{6,965},{7,966},{8... | collective-permute-start | bytes 589832 | tf_op jit(solution)/shard_map/ppermute | solution.py:253
  26.0 1.0 %copy-start.3 = (bf16[256,1024]{1,0:T(8,128)(2,1)S(1)}, bf16[256,1024]{1,0:T(8,128)(2,1)}, u32[]{:S(2)}) copy-start(bf16[256,1024]{1,0:T(8,128)(2,1)} %constant.9.clone.joined) | copy-start | bytes 1572868
  27.0 2.1 %copy-start.4 = (bf16[256,1024]{1,0:T(8,128)(2,1)S(1)}, bf16[256,1024]{1,0:T(8,128)(2,1)}, u32[]{:S(2)}) copy-start(bf16[256,1024]{1,0:T(8,128)(2,1)} %constant.9.clone.joined) | copy-start | bytes 1572868
  55.4 8.9 %collective-permute-start.3 = (f32[24,128]{1,0:T(8,128)S(1)}, f32[24,128]{1,0:T(8,128)S(1)}, u32[]{:S(2)}, u32[]{:S(2)}) collective-permute-start(f32[24,128]{1,0:T(8,128)S(1)} %slice.9), channel_id=1, source_target_pairs={{0,64},{1,65},{2,66},{3,67},{4,68},{5,69},{6,70},{7,71},{8,72},{9,... | collective-permute-start | bytes 36872 | tf_op jit(solution)/shard_map/ppermute | solution.py:253

commit v10 on v9

--- a/solution.py
+++ b/solution.py
@@ -229,21 +229,13 @@
     )(remote, trial, carried, other, mine, own, *tabs)
 
 
-LOW = 4
-
-
-def route(blocks, groups, distance, parity, cycle=False):
+def route(blocks, groups, distance, parity, turn):
     half = blocks // 2
     pairs = []
     for block in range(parity, blocks, 2):
         target = (block + distance) % blocks
         for group in range(groups):
-            place = group % LOW
-            if target // half != block // half:
-                place = LOW - 1 - place
-                if cycle:
-                    place = (group + (1 if block >= half else LOW - 1)) % LOW
-            place += group // LOW * LOW
+            place = group ^ turn if target // half != block // half else group
             pairs.append((block * groups + group, target * groups + place))
     return pairs
 
@@ -253,15 +245,15 @@
     send = lambda what, *how: lax.ppermute(what, ("orb", "grp"), route(blocks, groups, *how))
     tabs = tables()
     target = as_rows(targets)
-    remote = send(target, -2, 0, True)
+    remote = send(target, -2, 0, 3)
     partner = as_rows(partners)
-    carried = send(partner, 2, 1)
+    carried = send(partner, 2, 1, 2)
     other = lax.ppermute(partner, "orb", [(i ^ 1, i) for i in range(blocks)])
     own, mine = own_call(target, partner, tabs)
     fields = cross_call(remote, target, carried, other, mine, own, tabs)
     slabs = lax.all_to_all(fields, "grp", 0, 0, tiled=True)
     summed = jnp.sum(slabs.astype(f32), axis=0)
-    ahead = send(summed[HALF:], 2, 0)
+    ahead = send(summed[HALF:], 2, 0, 3)
     factor = -1.0 / math.sqrt(STEPS * groups * 2)
     return ((summed[:HALF] + ahead) * factor).reshape(1, Y * Z)
 

time: 65.3 us -> 64.3 us (0.985)
  blocking collectives: 23.9 us -> 22.2 us
  waiting for transfers between devices: 7.38 us -> 8.05 us
    all_to_all x1, blocking collectives: 23.9 us -> 22.2 us  [local(): slabs = lax.all_to_all(fields, 'grp', 0, 0, tiled=True)]
    ppermute x3, waiting for transfers between devices: 7.38 us -> 8.04 us  [local(): lax.ppermute(what, ('orb', 'grp'), route(blocks, groups, *how))]
where the time goes in v10:
time: 64.3 us; the launch traced here: 64 us
  starting transfers between devices  26.7 us (42%)
  blocking collectives  22.2 us (35%)
  waiting for transfers between devices  8.05 us (13%)
  Pallas kernels  4.16 us (6%)
  local copies, waits for them, and re-layouts  2.05 us (3%)
  other arithmetic  0.67 us (1%)
    ppermute x3, starting transfers between devices, local(): lax.ppermute(what, ('orb', 'grp'), route(blocks, groups, *how))  22.4 us
    all_to_all x1, blocking collectives, local(): slabs = lax.all_to_all(fields, 'grp', 0, 0, tiled=True)  22.2 us
    ppermute x3, waiting for transfers between devices, local(): lax.ppermute(what, ('orb', 'grp'), route(blocks, groups, *how))  8.04 us
    ppermute x1, starting transfers between devices, local(): other = lax.ppermute(partner, 'orb', [(i ^ 1, i) for i in range(blocks)])  4.38 us
    pallas_call x1, Pallas kernels, cross_call(): pl.pallas_call(cross_kernel, out_shape=jax.ShapeDtypeStruct((X, Y, 2 * Z)...  2.37 us
    unnamed x10, local copies, waits for them, and re-layouts  2.04 us
    pallas_call x1, Pallas kernels, own_call(): pl.pallas_call(own_kernel, out_shape=(jax.ShapeDtypeStruct((X, HALF, 2 *...  1.7 us
  transfers between devices with their start and end apart: 4, of which 2 were waited for; matrix products, arithmetic and copies ran while one was open for 0% of the time, Pallas kernels for 3%

profile of v10, /device:TPU:2, one launch (start us, length us, event | category | flops | bytes accessed | tf_op | source)
XLA Modules:
  0.0 64.0 jit_solution(15858383175790859353)
XLA Ops:
  0.0 0.0 copy-start
  0.0 1.0 %copy-done = bf16[2,98304]{1,0:T(2,128)(2,1)S(1)} copy-done((bf16[2,98304]{1,0:T(2,128)(2,1)S(1)}, bf16[2,98304]{1,0:T(2,128)(2,1)}, u32[]{:S(2)}) %copy-start) | copy-done | bytes 393240
  1.0 0.0 copy-start.1
  1.0 0.0 copy-start.2
  1.0 0.1 as_rows.3.p_ref
  1.1 0.8 %collective-permute-start.1 = (bf16[1536,128]{1,0:T(8,128)(2,1)S(1)}, bf16[1536,128]{1,0:T(8,128)(2,1)S(1)}, u32[]{:S(2)}, u32[]{:S(2)}) collective-permute-start(bf16[1536,128]{1,0:T(8,128)(2,1)S(1)} %as_rows.3.p_ref), channel_id=1, source_target_pairs={{32,96},{33,97},{34,98},{35,99},{36,100},{37,101},{38,102},{39,103... | collective-permute-start | bytes 1179656 | tf_op jit(solution)/shard_map/ppermute | solution.py:245
  1.9 4.4 %collective-permute-start.2 = (bf16[1536,128]{1,0:T(8,128)(2,1)S(1)}, bf16[1536,128]{1,0:T(8,128)(2,1)S(1)}, u32[]{:S(2)}, u32[]{:S(2)}) collective-permute-start(bf16[1536,128]{1,0:T(8,128)(2,1)S(1)} %as_rows.3.p_ref), channel_id=1, source_target_pairs={{32,0},{0,32},{96,64},{64,96},{160,128},{128,160},{224,192},{192,2... | collective-permute-start | bytes 1179656 | tf_op jit(solution)/shard_map/ppermute | solution.py:251
  6.3 0.0 copy-done.1
  6.3 19.6 %collective-permute-start = (bf16[768,128]{1,0:T(8,128)(2,1)S(1)}, bf16[768,128]{1,0:T(8,128)(2,1)S(1)}, u32[]{:S(2)}, u32[]{:S(2)}) collective-permute-start(bf16[768,128]{1,0:T(8,128)(2,1)S(1)} %as_rows.2.t_ref), channel_id=1, source_target_pairs={{0,963},{1,962},{2,961},{3,960},{4,967},{5,966},{6,965},{7,964},{8... | collective-permute-start | bytes 589832 | tf_op jit(solution)/shard_map/ppermute | solution.py:245
  25.9 0.0 copy-done.2
  26.0 0.0 copy-start.3
  26.0 1.0 %copy-done.3 = bf16[256,1024]{1,0:T(8,128)(2,1)S(1)} copy-done((bf16[256,1024]{1,0:T(8,128)(2,1)S(1)}, bf16[256,1024]{1,0:T(8,128)(2,1)}, u32[]{:S(2)}) %copy-start.3) | copy-done | bytes 524312
  27.0 0.0 copy-start.4
  27.0 1.7 %own_terms.1 = (f32[32,24,128]{2,1,0:T(8,128)S(1)}, bf16[1536,128]{1,0:T(8,128)(2,1)S(1)}) custom-call(bf16[768,128]{1,0:T(8,128)(2,1)S(1)} %as_rows.2.t_ref, bf16[1536,128]{1,0:T(8,128)(2,1)S(1)} %as_rows.3.p_ref, bf16[256,1024]{1,0:T(8,128)(2,1)S(1)} %copy-done.3, f32[32,48,128]{2,1,0:T(8,128)S(1)} %copy-done.2), custom_call_target="tpu_custom_call" | custom-call | flops 4000000000 | bytes 3000000 | tf_op jit(solution)/shard_map/own_terms/pallas_call | solution.py:204
  28.7 0.4 collective-permute-done.r_ref
  29.1 0.0 collective-permute-done.1.c_ref
  29.1 0.0 collective-permute-done.2.q_ref
  29.1 0.0 copy-done.4
  29.1 2.4 %cross_terms.1 = bf16[32,48,128]{2,1,0:T(8,128)(2,1)S(1)} custom-call(bf16[768,128]{1,0:T(8,128)(2,1)S(1)} %collective-permute-done.r_ref, bf16[768,128]{1,0:T(8,128)(2,1)S(1)} %as_rows.2.t_ref, bf16[1536,128]{1,0:T(8,128)(2,1)S(1)} %collective-permute-done.1.c_ref, bf16[1536,128]{1,0:T(8,128)(2,1)S(1)} %collective-permute-done.2.q_ref, ...), custom_call_target="tpu_custom_call" | custom-call | flops 4000000000 | bytes 3000000 | tf_op jit(solution)/shard_map/cross_terms/pallas_call | solution.py:220
  31.5 22.2 %all_to_all.5 = bf16[32,48,128]{2,1,0:T(8,128)(2,1)S(1)} all-to-all(bf16[32,48,128]{2,1,0:T(8,128)(2,1)S(1)} %cross_terms.1), channel_id=1, replica_groups=mesh['orb'=32,'grp'=32] {'grp'}, dimensions={0} | all-to-all | bytes 786432 | tf_op jit(solution)/shard_map/all_to_all | solution.py:254
  53.7 0.1 convert_reduce_fusion
  53.8 1.9 %collective-permute-start.3 = (f32[24,128]{1,0:T(8,128)S(1)}, f32[24,128]{1,0:T(8,128)S(1)}, u32[]{:S(2)}, u32[]{:S(2)}) collective-permute-start(f32[24,128]{1,0:T(8,128)S(1)} %slice.9), channel_id=1, source_target_pairs={{0,64},{1,65},{2,66},{3,67},{4,68},{5,69},{6,70},{7,71},{8,72},{9,... | collective-permute-start | bytes 36872 | tf_op jit(solution)/shard_map/ppermute | solution.py:245
  55.7 7.6 %collective-permute-done.3 = f32[24,128]{1,0:T(8,128)S(1)} collective-permute-done((f32[24,128]{1,0:T(8,128)S(1)}, f32[24,128]{1,0:T(8,128)S(1)}, u32[]{:S(2)}, u32[]{:S(2)}) %collective-permute-start.3) | collective-permute-done | bytes 12320 | tf_op jit(solution)/shard_map/ppermute | solution.py:245
  63.4 0.6 fusion
  (2 shorter events, 0.0 us)
Async XLA Ops:
  0.0 1.0 %copy-start = (bf16[2,98304]{1,0:T(2,128)(2,1)S(1)}, bf16[2,98304]{1,0:T(2,128)(2,1)}, u32[]{:S(2)}) copy-start(bf16[2,98304]{1,0:T(2,128)(2,1)} %x_ref.3) | copy-start | bytes 1179652
  1.0 5.3 %copy-start.1 = (bf16[1,98304]{1,0:T(2,128)(2,1)S(1)}, bf16[1,98304]{1,0:T(2,128)(2,1)}, u32[]{:S(2)}) copy-start(bf16[1,98304]{1,0:T(2,128)(2,1)} %x_ref.2) | copy-start | bytes 589828
  1.0 24.9 %copy-start.2 = (f32[32,48,128]{2,1,0:T(8,128)S(1)}, f32[32,48,128]{2,1,0:T(8,128)}, u32[]{:S(2)}) copy-start(f32[32,48,128]{2,1,0:T(8,128)} %constant.8.clone.kernel) | copy-start | bytes 2359300
  1.1 28.1 %collective-permute-start.1 = (bf16[1536,128]{1,0:T(8,128)(2,1)S(1)}, bf16[1536,128]{1,0:T(8,128)(2,1)S(1)}, u32[]{:S(2)}, u32[]{:S(2)}) collective-permute-start(bf16[1536,128]{1,0:T(8,128)(2,1)S(1)} %as_rows.3.p_ref), channel_id=1, source_target_pairs={{32,96},{33,97},{34,98},{35,99},{36,100},{37,101},{38,102},{39,103... | collective-permute-start | bytes 1179656 | tf_op jit(solution)/shard_map/ppermute | solution.py:245
  1.9 27.2 %collective-permute-start.2 = (bf16[1536,128]{1,0:T(8,128)(2,1)S(1)}, bf16[1536,128]{1,0:T(8,128)(2,1)S(1)}, u32[]{:S(2)}, u32[]{:S(2)}) collective-permute-start(bf16[1536,128]{1,0:T(8,128)(2,1)S(1)} %as_rows.3.p_ref), channel_id=1, source_target_pairs={{32,0},{0,32},{96,64},{64,96},{160,128},{128,160},{224,192},{192,2... | collective-permute-start | bytes 1179656 | tf_op jit(solution)/shard_map/ppermute | solution.py:251
  6.3 22.8 %collective-permute-start = (bf16[768,128]{1,0:T(8,128)(2,1)S(1)}, bf16[768,128]{1,0:T(8,128)(2,1)S(1)}, u32[]{:S(2)}, u32[]{:S(2)}) collective-permute-start(bf16[768,128]{1,0:T(8,128)(2,1)S(1)} %as_rows.2.t_ref), channel_id=1, source_target_pairs={{0,963},{1,962},{2,961},{3,960},{4,967},{5,966},{6,965},{7,964},{8... | collective-permute-start | bytes 589832 | tf_op jit(solution)/shard_map/ppermute | solution.py:245
  26.0 1.0 %copy-start.3 = (bf16[256,1024]{1,0:T(8,128)(2,1)S(1)}, bf16[256,1024]{1,0:T(8,128)(2,1)}, u32[]{:S(2)}) copy-start(bf16[256,1024]{1,0:T(8,128)(2,1)} %constant.9.clone.joined) | copy-start | bytes 1572868
  27.0 2.1 %copy-start.4 = (bf16[256,1024]{1,0:T(8,128)(2,1)S(1)}, bf16[256,1024]{1,0:T(8,128)(2,1)}, u32[]{:S(2)}) copy-start(bf16[256,1024]{1,0:T(8,128)(2,1)} %constant.9.clone.joined) | copy-start | bytes 1572868
  53.8 9.6 %collective-permute-start.3 = (f32[24,128]{1,0:T(8,128)S(1)}, f32[24,128]{1,0:T(8,128)S(1)}, u32[]{:S(2)}, u32[]{:S(2)}) collective-permute-start(f32[24,128]{1,0:T(8,128)S(1)} %slice.9), channel_id=1, source_target_pairs={{0,64},{1,65},{2,66},{3,67},{4,68},{5,69},{6,70},{7,71},{8,72},{9,... | collective-permute-start | bytes 36872 | tf_op jit(solution)/shard_map/ppermute | solution.py:245
